TPU v7x, 256 devices: a whole 4x4x8 slice. The times are simulated.
256 devices in a mesh: wide: 32 (over z, y), narrow: 8 (over x, core).
Axes of the slice: x: 4, y: 4, z: 8, core: 2. Of those that a mesh axis runs over, the one named last changes fastest.
Arguments:
- upstream_hot: bfloat16 [524288, 512], P(('wide', 'narrow')), may hold values from -6 to 6
- upstream_warm: bfloat16 [524288, 512], P(('wide', 'narrow')), may hold values from -6 to 6
- upstream_cold: bfloat16 [524288, 512], P(('wide', 'narrow')), may hold values from -6 to 6
- saved_hot: bfloat16 [524288, 512], P(('wide', 'narrow')), may hold values from -6 to 6
- saved_warm: bfloat16 [524288, 128], P(('wide', 'narrow')), may hold values from -6 to 6
- saved_cold: bfloat16 [32, 524288], P(None, ('wide', 'narrow')), may hold values from -6 to 6
- weight_hot: bfloat16 [512, 512], replicated, may hold values from -0.25 to 0.25
- weight_warm: bfloat16 [128, 512], replicated, may hold values from -0.25 to 0.25
- weight_cold: bfloat16 [32, 512], replicated, may hold values from -0.25 to 0.25
- owner_hot: int32 [524288, 1], P(('wide', 'narrow')), may hold values from 0 to 255; in each aligned block of 2048 rows (0 to 2047, 2048 to 4095, ...) at most 16 rows name the same one
- owner_warm: int32 [524288, 1], P(('wide', 'narrow')), may hold values from 0 to 255; in each aligned block of 2048 rows (0 to 2047, 2048 to 4095, ...) at most 16 rows name the same one
- owner_cold: int32 [524288, 1], P(('wide', 'narrow')), may hold values from 0 to 255; in each aligned block of 2048 rows (0 to 2047, 2048 to 4095, ...) at most 16 rows name the same one
- local_hot: int32 [524288], P(('wide', 'narrow')), may hold values from 0 to 511
- local_warm: int32 [524288], P(('wide', 'narrow')), may hold values from 0 to 2047
- local_cold: int32 [524288], P(('wide', 'narrow')), may hold values from 0 to 4095
Outputs:
- table_hot: float32 [131072, 512], P(('wide', 'narrow'))
- table_warm: float32 [524288, 128], P(('wide', 'narrow'))
- table_cold: float32 [32, 1048576], P(None, ('wide', 'narrow'))
- mixing_hot: float32 [512, 512], replicated
- mixing_warm: float32 [128, 512], replicated
- mixing_cold: float32 [32, 512], replicated
Inputs may be any that keep to these rules, and one draw needn't show every extreme that they name: `owner_hot`: among the 2048 lookups of the most frequent bucket on one device, at most 16 have the same owner, and that many is reached. `owner_warm`: among the 2048 lookups of the middle bucket on one device, at most 16 have the same owner, and that many is reached. `owner_cold`: among the 2048 lookups of the rarest bucket on one device, at most 16 have the same owner, and that many is reached.
All inputs are finite; a program needn't handle non-finite values.
Results may differ from a plain program's by a relative error of at most 0.0029.
Values may be sent and summed in bfloat16 or wider, within the bound.
A program may use at most 128 MiB of HBM per device.

v0:
```python
import math

import jax
import jax.numpy as jnp
from jax import lax
from jax.sharding import PartitionSpec as P

W_HOT = 512
W_WARM = 128
W_COLD = 32
LOOK = 2048
ROWS_HOT = 512
ROWS_WARM = 2048
ROWS_COLD = 4096


def project(values, weight):
    return lax.dot_general(
        values, weight, (((1,), (1,)), ((), ())), preferred_element_type=jnp.float32
    )


def pack_rows(values, owners, local_rows, capacity, devices, narrow_size):
    targets = lax.iota(jnp.int32, devices)
    onehot = (owners[:, None] == targets[None, :]).astype(jnp.int32)
    position = jnp.sum(jnp.cumsum(onehot, axis=0) * onehot, axis=1) - 1
    placed = owners * capacity + position
    columns = values.shape[1]
    buffer = jnp.zeros((devices * capacity, columns), values.dtype).at[placed].set(values)
    labels = jnp.full((devices * capacity,), -1, jnp.int32).at[placed].set(local_rows)
    wide_size = devices // narrow_size
    return (
        buffer.reshape(wide_size, narrow_size, capacity * columns),
        labels.reshape(wide_size, narrow_size, capacity),
    )


def segment_rows(terms, labels, table_rows, transposed):
    block_rows = min(512, table_rows)
    flat_labels = labels.reshape(-1)

    def one_block(start):
        index_rows = start + lax.iota(jnp.int32, block_rows)
        if transposed:
            onehot = (flat_labels[:, None] == index_rows[None, :]).astype(jnp.bfloat16)
            return lax.dot_general(
                terms, onehot, (((0,), (0,)), ((), ())), preferred_element_type=jnp.float32
            )
        onehot = (index_rows[:, None] == flat_labels[None, :]).astype(jnp.bfloat16)
        return jnp.dot(onehot, terms, preferred_element_type=jnp.float32)

    starts = jnp.arange(table_rows // block_rows, dtype=jnp.int32) * block_rows
    blocks = lax.map(one_block, starts)
    if transposed:
        return jnp.transpose(blocks, (1, 0, 2)).reshape(terms.shape[1], table_rows)
    return blocks.reshape(table_rows, terms.shape[1])


def per_device(
    upstream_hot,
    upstream_warm,
    upstream_cold,
    saved_hot,
    saved_warm,
    saved_cold,
    weight_hot,
    weight_warm,
    weight_cold,
    owner_hot,
    owner_warm,
    owner_cold,
    local_hot,
    local_warm,
    local_cold,
):
    narrow_size = lax.axis_size("narrow")
    devices = lax.axis_size("wide") * narrow_size
    capacity = max(2, 2 * LOOK // devices)
    sent_hot, label_hot = pack_rows(
        project(upstream_hot, weight_hot).astype(jnp.bfloat16),
        owner_hot[:, 0],
        local_hot,
        capacity,
        devices,
        narrow_size,
    )
    sent_warm, label_warm = pack_rows(
        project(upstream_warm, weight_warm).astype(jnp.bfloat16),
        owner_warm[:, 0],
        local_warm,
        capacity,
        devices,
        narrow_size,
    )
    sent_cold, label_cold = pack_rows(
        project(upstream_cold, weight_cold).astype(jnp.bfloat16),
        owner_cold[:, 0],
        local_cold,
        capacity,
        devices,
        narrow_size,
    )
    got_hot, got_warm, got_cold, lab_hot, lab_warm, lab_cold = (
        lax.all_to_all(
            lax.all_to_all(sent_hot, "wide", split_axis=0, concat_axis=0, tiled=True),
            "narrow",
            split_axis=1,
            concat_axis=1,
            tiled=True,
        ),
        lax.all_to_all(
            lax.all_to_all(sent_warm, "wide", split_axis=0, concat_axis=0, tiled=True),
            "narrow",
            split_axis=1,
            concat_axis=1,
            tiled=True,
        ),
        lax.all_to_all(
            lax.all_to_all(sent_cold, "wide", split_axis=0, concat_axis=0, tiled=True),
            "narrow",
            split_axis=1,
            concat_axis=1,
            tiled=True,
        ),
        lax.all_to_all(
            lax.all_to_all(label_hot, "wide", split_axis=0, concat_axis=0, tiled=True),
            "narrow",
            split_axis=1,
            concat_axis=1,
            tiled=True,
        ),
        lax.all_to_all(
            lax.all_to_all(label_warm, "wide", split_axis=0, concat_axis=0, tiled=True),
            "narrow",
            split_axis=1,
            concat_axis=1,
            tiled=True,
        ),
        lax.all_to_all(
            lax.all_to_all(label_cold, "wide", split_axis=0, concat_axis=0, tiled=True),
            "narrow",
            split_axis=1,
            concat_axis=1,
            tiled=True,
        ),
    )
    term_hot = got_hot.reshape(-1, W_HOT)
    term_warm = got_warm.reshape(-1, W_WARM)
    term_cold = got_cold.reshape(-1, W_COLD)
    table_hot = segment_rows(term_hot, lab_hot, ROWS_HOT, False)
    table_warm = segment_rows(term_warm, lab_warm, ROWS_WARM, False)
    table_cold = segment_rows(term_cold, lab_cold, ROWS_COLD, True)
    part_hot = lax.dot_general(
        saved_hot, upstream_hot, (((0,), (0,)), ((), ())), preferred_element_type=jnp.float32
    )
    part_warm = lax.dot_general(
        saved_warm, upstream_warm, (((0,), (0,)), ((), ())), preferred_element_type=jnp.float32
    )
    part_cold = jnp.dot(saved_cold, upstream_cold, preferred_element_type=jnp.float32)
    factor = 1.0 / math.sqrt(LOOK * devices)
    total_hot, total_warm, total_cold = lax.psum(
        (part_hot, part_warm, part_cold), ("wide", "narrow")
    )
    return (
        table_hot,
        table_warm,
        table_cold,
        total_hot * factor,
        total_warm * factor,
        total_cold * factor,
    )


def solution(mesh):
    placed = (
        P(("wide", "narrow"), None),
        P(("wide", "narrow"), None),
        P(("wide", "narrow"), None),
        P(("wide", "narrow"), None),
        P(("wide", "narrow"), None),
        P(None, ("wide", "narrow")),
        P(),
        P(),
        P(),
        P(("wide", "narrow"), None),
        P(("wide", "narrow"), None),
        P(("wide", "narrow"), None),
        P(("wide", "narrow")),
        P(("wide", "narrow")),
        P(("wide", "narrow")),
    )
    return jax.shard_map(
        per_device,
        mesh=mesh,
        in_specs=placed,
        out_specs=(
            P(("wide", "narrow"), None),
            P(("wide", "narrow"), None),
            P(None, ("wide", "narrow")),
            P(),
            P(),
            P(),
        ),
        check_vma=False,
    )
```

profile of v0, /device:TPU:2, one launch (start us, length us, event | category | flops | bytes accessed | tf_op | source)
XLA Modules:
  0.0 583.7 jit_solution(10837068983426819529)
XLA Ops:
  14.5 8.2 %scatter_custom_fusion = s32[4096]{0:T(1024)S(1)} fusion(s32[2048]{0:T(1024)S(1)} %bitcast.108, s32[2048]{0:T(1024)} %param.31, s32[]{:T(128)} %constant.28.clone.1), kind=kCustom, calls=%fused_computation.69 | custom fusion | bytes 16896 | tf_op jit(solution)/shard_map/scatter | solution.py:30
  23.5 11.5 %all-to-all-start = ((s32[32,1,128]{2,1,0:T(1,128)}), s32[32,1,128]{2,1,0:T(1,128)S(1)}, u32[]{:S(2)}, u32[]{:S(2)}) async-start(s32[32,1,128]{2,1,0:T(1,128)} %reshape.208), calls=%async_computation | async-start | bytes 32768 | tf_op jit(solution)/shard_map/all_to_all | solution.py:126
  46.7 8.2 %scatter_custom_fusion.2 = s32[4096]{0:T(1024)S(1)} fusion(s32[2048]{0:T(1024)S(1)} %bitcast.110, s32[2048]{0:T(1024)} %param.32, s32[]{:T(128)} %constant.28.clone.1), kind=kCustom, calls=%fused_computation.67 | custom fusion | bytes 16896 | tf_op jit(solution)/shard_map/scatter | solution.py:30
  55.8 9.8 %all-to-all-start.4 = ((s32[32,1,128]{2,1,0:T(1,128)}), s32[32,1,128]{2,1,0:T(1,128)S(1)}, u32[]{:S(2)}, u32[]{:S(2)}) async-start(s32[32,1,128]{2,1,0:T(1,128)} %reshape.212), calls=%async_computation.4 | async-start | bytes 32768 | tf_op jit(solution)/shard_map/all_to_all | solution.py:133
  65.6 8.2 %scatter_custom_fusion.4 = s32[4096]{0:T(1024)S(1)} fusion(s32[2048]{0:T(1024)S(1)} %bitcast.112, s32[2048]{0:T(1024)} %param.33, s32[]{:T(128)} %constant.28.clone.1), kind=kCustom, calls=%fused_computation.65 | custom fusion | bytes 16896 | tf_op jit(solution)/shard_map/scatter | solution.py:30
  75.3 9.2 %all-to-all-start.8 = ((s32[32,1,128]{2,1,0:T(1,128)}), s32[32,1,128]{2,1,0:T(1,128)S(1)}, u32[]{:S(2)}, u32[]{:S(2)}) async-start(s32[32,1,128]{2,1,0:T(1,128)} %reshape.216), calls=%async_computation.8 | async-start | bytes 32768 | tf_op jit(solution)/shard_map/all_to_all | solution.py:140
  86.6 7.6 %all-to-all-done.8 = s32[32,1,128]{2,1,0:T(1,128)S(1)} async-done(((s32[32,1,128]{2,1,0:T(1,128)}), s32[32,1,128]{2,1,0:T(1,128)S(1)}, u32[]{:S(2)}, u32[]{:S(2)}) %all-to-all-start.8) | async-done | bytes 16416 | tf_op jit(solution)/shard_map/all_to_all | solution.py:140
  94.1 4.8 all-to-all-start.1
  102.9 4.7 all-to-all-start.5
  110.9 6.4 %scatter_custom_fusion.5 = bf16[4096,32]{1,0:T(8,128)(2,1)S(1)} fusion(s32[2048]{0:T(1024)S(1)} %bitcast.113, bf16[2048,32]{1,0:T(8,128)(2,1)} %copy.64, bf16[]{:T(256)} %constant.37.clone.1), kind=kCustom, calls=%fused_computation.53 | custom fusion | bytes 262656 | tf_op jit(solution)/shard_map/scatter | solution.py:29
  119.0 3.9 all-to-all-start.10
  124.5 11.9 %all-to-all-done.10 = bf16[32,8,512]{2,1,0:T(8,128)(2,1)S(1)} async-done(((bf16[32,8,512]{2,1,0:T(8,128)(2,1)}), bf16[32,8,512]{2,1,0:T(8,128)(2,1)S(1)}, u32[]{:S(2)}, u32[]{:S(2)}) %all-to-all-start.10) | async-done | bytes 262176 | tf_op jit(solution)/shard_map/all_to_all | solution.py:119
  136.4 4.8 all-to-all-start.9
  145.7 4.8 all-to-all-start.11
  153.6 6.4 %scatter_custom_fusion.3 = bf16[4096,128]{1,0:T(8,128)(2,1)S(1)} fusion(s32[2048]{0:T(1024)} %bitcast.111, bf16[2048,128]{1,0:T(8,128)(2,1)} %convolution_convert_fusion.1, bf16[]{:T(256)} %constant.37.clone.1), kind=kCustom, calls=%fused_computation.55 | custom fusion | bytes 1049088 | tf_op jit(solution)/shard_map/scatter | solution.py:29
  161.3 4.1 all-to-all-start.6
  165.4 3.7 convolution_convert_fusion
  169.1 12.6 %scatter_custom_fusion.1 = bf16[4096,512]{1,0:T(8,128)(2,1)} fusion(s32[2048]{0:T(1024)} %bitcast.109, bf16[2048,512]{1,0:T(8,128)(2,1)} %convolution_convert_fusion, bf16[]{:T(256)} %constant.37.clone.1), kind=kCustom, calls=%fused_computation.40 | custom fusion | bytes 4194816 | tf_op jit(solution)/shard_map/scatter | solution.py:29
  181.6 7.4 %reshape.136 = bf16[32,8,8192]{2,1,0:T(8,128)(2,1)} reshape(bf16[4096,512]{1,0:T(8,128)(2,1)} %scatter_custom_fusion.1) | data formatting | bytes 8388608 | tf_op jit(solution)/shard_map/reshape | solution.py:33
  189.1 5.3 all-to-all-done.6
  194.3 5.4 all-to-all-start.2
  208.7 88.8 %all-to-all-done.2 = bf16[32,8,8192]{2,1,0:T(8,128)(2,1)} async-done(((bf16[32,8,8192]{2,1,0:T(8,128)(2,1)}), bf16[32,8,8192]{2,1,0:T(8,128)(2,1)}, u32[]{:S(2)}, u32[]{:S(2)}) %all-to-all-start.2) | async-done | bytes 4194336 | tf_op jit(solution)/shard_map/all_to_all | solution.py:105
  297.6 4.8 all-to-all-start.7
  305.3 185.6 %all-reduce.3.cloned.1.call-done = (f32[512,512]{1,0:T(8,128)}, f32[128,512]{1,0:T(8,128)}, f32[32,512]{1,0:T(8,128)}) async-done(((f32[512,512]{1,0:T(8,128)}, f32[128,512]{1,0:T(8,128)}, f32[32,512]{1,0:T(8,128)}), (f32[512,512]{1,0:T(8,128)}, f32[128,512]{1,0:T(8,128)}, f32[32,512]{1,0:T(8,128)})) %all-reduce.3.cloned.1.call-update) | async-done | bytes 1376272 | tf_op jit(solution)/shard_map/psum | solution.py:161
  497.1 6.5 %copy.53 = bf16[32,8,8192]{2,0,1:T(8,128)(2,1)} copy(bf16[32,8,8192]{2,1,0:T(8,128)(2,1)} %all-to-all-done.2) | data formatting | bytes 8388608 | tf_op jit(solution)/shard_map/all_to_all | solution.py:105
  503.6 5.3 all-to-all-start.3
  508.9 23.5 %while.27 = (s32[]{:T(128)}, f32[8,32,512]{2,1,0:T(8,128)S(1)}, s32[32,8,16]{2,1,0:T(8,128)}, s32[8]{0:T(128)S(1)}, bf16[4096,32]{1,0:T(8,128)(2,1)S(1)}, /*index=5*/s32[4096]{0:T(1024)S(1)}, s32[]{:T(128)}) while((s32[]{:T(128)}, f32[8,32,512]{2,1,0:T(8,128)S(1)}, s32[32,8,16]{2,1,0:T(8,128)}, s32[8]{0:T(128)S(1)}, ...), condition=%wide.wide.region_18.19_spmd, body=%wide.wide.region_17.18_spmd.sunk | while | flops 136315392 | bytes 1134697 | solution.py:53
  534.4 13.0 %while.26 = (s32[]{:T(128)}, f32[4,512,128]{2,1,0:T(8,128)}, s32[4]{0:T(128)S(1)}, s32[32,8,16]{2,1,0:T(8,128)}, bf16[4096,128]{1,0:T(8,128)(2,1)S(1)}, /*index=5*/s32[4096]{0:T(1024)S(1)}, s32[]{:T(128)}) while((s32[]{:T(128)}, f32[4,512,128]{2,1,0:T(8,128)}, s32[4]{0:T(128)S(1)}, s32[32,8,16]{2,1,0:T(8,128)}, ...), condition=%wide.wide.region_11.12_spmd, body=%wide.wide.region_10.11_spmd.sunk | while | flops 538968576 | bytes 1331305 | solution.py:53
  547.4 9.7 %all-to-all-done.3 = bf16[32,8,8192]{2,0,1:T(8,128)(2,1)} async-done(((bf16[32,8,8192]{2,0,1:T(8,128)(2,1)}), bf16[32,8,8192]{2,0,1:T(8,128)(2,1)}, u32[]{:S(2)}, u32[]{:S(2)}) %all-to-all-start.3) | async-done | bytes 4194336 | tf_op jit(solution)/shard_map/all_to_all | solution.py:104
  557.1 6.5 %copy.54 = bf16[32,8,8192]{2,1,0:T(8,128)(2,1)} copy(bf16[32,8,8192]{2,0,1:T(8,128)(2,1)} %all-to-all-done.3) | data formatting | bytes 8388608 | tf_op jit(solution)/shard_map/all_to_all | solution.py:104
  563.6 7.4 %reshape.137 = bf16[4096,512]{1,0:T(8,128)(2,1)} reshape(bf16[32,8,8192]{2,1,0:T(8,128)(2,1)} %copy.54) | data formatting | bytes 8388608 | tf_op jit(solution)/shard_map/reshape | solution.py:147
  571.0 5.6 fusion.20
  (172 shorter events, 99.7 us)
Async XLA Ops:
  7.2 158.3 %copy-start = (bf16[2048,512]{1,0:T(8,128)(2,1)S(1)}, bf16[2048,512]{1,0:T(8,128)(2,1)}, u32[]{:S(2)}) copy-start(bf16[2048,512]{1,0:T(8,128)(2,1)} %param.19) | copy-start | bytes 6291460
  8.5 1.4 copy-start.2
  11.7 1.3 copy-start.11
  12.9 22.1 %copy-start.12 = (s32[2048,1]{0,1:T(1,128)S(1)}, s32[2048,1]{0,1:T(1,128)}, u32[]{:S(2)}) copy-start(s32[2048,1]{0,1:T(1,128)} %param.29) | copy-start | bytes 24580
  23.5 32.3 %all-to-all-start = ((s32[32,1,128]{2,1,0:T(1,128)}), s32[32,1,128]{2,1,0:T(1,128)S(1)}, u32[]{:S(2)}, u32[]{:S(2)}) async-start(s32[32,1,128]{2,1,0:T(1,128)} %reshape.208), calls=%async_computation | async-start | bytes 32768 | tf_op jit(solution)/shard_map/all_to_all | solution.py:126
  35.5 1.4 copy-start.3
  40.9 5.8 %copy-start.20 = (s32[2048,1]{0,1:T(1,128)}, s32[2048,1]{0,1:T(1,128)S(1)}, u32[]{:S(2)}) copy-start(s32[2048,1]{0,1:T(1,128)S(1)} %compare_select_fusion.1) | copy-start | bytes 24580
  41.4 1.4 copy-start.4
  45.8 61.8 %copy-start.18 = (bf16[32,512]{1,0:T(8,128)(2,1)S(1)}, bf16[32,512]{1,0:T(8,128)(2,1)}, u32[]{:S(2)}) copy-start(bf16[32,512]{1,0:T(8,128)(2,1)} %param.27) | copy-start | bytes 98308
  55.8 19.5 %all-to-all-start.4 = ((s32[32,1,128]{2,1,0:T(1,128)}), s32[32,1,128]{2,1,0:T(1,128)S(1)}, u32[]{:S(2)}, u32[]{:S(2)}) async-start(s32[32,1,128]{2,1,0:T(1,128)} %reshape.212), calls=%async_computation.4 | async-start | bytes 32768 | tf_op jit(solution)/shard_map/all_to_all | solution.py:133
  75.3 18.9 %all-to-all-start.8 = ((s32[32,1,128]{2,1,0:T(1,128)}), s32[32,1,128]{2,1,0:T(1,128)S(1)}, u32[]{:S(2)}, u32[]{:S(2)}) async-start(s32[32,1,128]{2,1,0:T(1,128)} %reshape.216), calls=%async_computation.8 | async-start | bytes 32768 | tf_op jit(solution)/shard_map/all_to_all | solution.py:140
  94.1 8.7 %all-to-all-start.1 = ((s32[8,1,512]{2,1,0:T(1,128)}), s32[8,1,512]{2,1,0:T(1,128)S(1)}, u32[]{:S(2)}, u32[]{:S(2)}) async-start(s32[8,1,512]{2,1,0:T(1,128)} %reshape.210), calls=%async_computation.1 | async-start | bytes 32768 | tf_op jit(solution)/shard_map/all_to_all | solution.py:125
  102.9 16.1 %all-to-all-start.5 = ((s32[8,1,512]{2,1,0:T(1,128)}), s32[8,1,512]{2,1,0:T(1,128)S(1)}, u32[]{:S(2)}, u32[]{:S(2)}) async-start(s32[8,1,512]{2,1,0:T(1,128)} %reshape.214), calls=%async_computation.5 | async-start | bytes 32768 | tf_op jit(solution)/shard_map/all_to_all | solution.py:132
  110.9 39.6 %copy-start.10 = (bf16[128,512]{1,0:T(8,128)(2,1)S(1)}, bf16[128,512]{1,0:T(8,128)(2,1)}, u32[]{:S(2)}) copy-start(bf16[128,512]{1,0:T(8,128)(2,1)} %param.26) | copy-start | bytes 393220
  119.0 26.1 %copy-start.14 = (s32[8,1,512]{2,1,0:T(1,128)}, s32[8,1,512]{2,1,0:T(1,128)S(1)}, u32[]{:S(2)}) copy-start(s32[8,1,512]{2,1,0:T(1,128)S(1)} %all-to-all-done.5) | copy-start | bytes 49156
  119.0 17.4 %all-to-all-start.10 = ((bf16[32,8,512]{2,1,0:T(8,128)(2,1)}), bf16[32,8,512]{2,1,0:T(8,128)(2,1)S(1)}, u32[]{:S(2)}, u32[]{:S(2)}) async-start(bf16[32,8,512]{2,1,0:T(8,128)(2,1)} %reshape.145), calls=%async_computation.10 | async-start | bytes 524288 | tf_op jit(solution)/shard_map/all_to_all | solution.py:119
  136.4 8.7 %all-to-all-start.9 = ((s32[8,1,512]{2,1,0:T(1,128)}), s32[8,1,512]{2,1,0:T(1,128)S(1)}, u32[]{:S(2)}, u32[]{:S(2)}) async-start(s32[8,1,512]{2,1,0:T(1,128)} %reshape.218), calls=%async_computation.9 | async-start | bytes 32768 | tf_op jit(solution)/shard_map/all_to_all | solution.py:139
  145.7 15.6 %all-to-all-start.11 = ((bf16[32,8,512]{2,0,1:T(8,128)(2,1)}), bf16[32,8,512]{2,0,1:T(8,128)(2,1)S(1)}, u32[]{:S(2)}, u32[]{:S(2)}) async-start(bf16[32,8,512]{2,0,1:T(8,128)(2,1)} %copy.65), calls=%async_computation.11 | async-start | bytes 524288 | tf_op jit(solution)/shard_map/all_to_all | solution.py:118
  161.3 33.0 %all-to-all-start.6 = ((bf16[32,8,2048]{2,1,0:T(8,128)(2,1)}), bf16[32,8,2048]{2,1,0:T(8,128)(2,1)S(1)}, u32[]{:S(2)}, u32[]{:S(2)}) async-start(bf16[32,8,2048]{2,1,0:T(8,128)(2,1)} %reshape.140), calls=%async_computation.6 | async-start | bytes 2097152 | tf_op jit(solution)/shard_map/all_to_all | solution.py:112
  189.0 10.7 %copy-start.9 = (bf16[32,2048]{1,0:T(8,128)(2,1)S(1)}, bf16[32,2048]{1,0:T(8,128)(2,1)}, u32[]{:S(2)}) copy-start(bf16[32,2048]{1,0:T(8,128)(2,1)} %param.24) | copy-start | bytes 393220
  194.3 103.2 %all-to-all-start.2 = ((bf16[32,8,8192]{2,1,0:T(8,128)(2,1)}), bf16[32,8,8192]{2,1,0:T(8,128)(2,1)}, u32[]{:S(2)}, u32[]{:S(2)}) async-start(bf16[32,8,8192]{2,1,0:T(8,128)(2,1)} %reshape.136), calls=%async_computation.2 | async-start | bytes 8388608 | tf_op jit(solution)/shard_map/all_to_all | solution.py:105
  199.7 291.2 %all-reduce.3.cloned.1.call-start = ((), (), s32[]{:S(2)}) async-start(), calls=%async_computation.12 | async-start | bytes 2752512 | tf_op jit(solution)/shard_map/psum | solution.py:161
  199.8 2.9 copy-start.5
  199.8 5.1 copy-start.21
  207.1 96.2 %copy-start.15 = (s32[8,1,512]{2,1,0:T(1,128)S(1)}, s32[8,1,512]{2,1,0:T(1,128)}, u32[]{:S(2)}) copy-start(s32[8,1,512]{2,1,0:T(1,128)} %copy-done.14) | copy-start | bytes 49156
  207.2 97.2 %copy-start.17 = (s32[8,1,512]{2,1,0:T(1,128)S(1)}, s32[8,1,512]{2,1,0:T(1,128)}, u32[]{:S(2)}) copy-start(s32[8,1,512]{2,1,0:T(1,128)} %copy-done.16) | copy-start | bytes 49156
  297.6 206.0 %all-to-all-start.7 = ((bf16[32,8,2048]{2,0,1:T(8,128)(2,1)}), bf16[32,8,2048]{2,0,1:T(8,128)(2,1)S(1)}, u32[]{:S(2)}, u32[]{:S(2)}) async-start(bf16[32,8,2048]{2,0,1:T(8,128)(2,1)} %copy.58), calls=%async_computation.7 | async-start | bytes 2097152 | tf_op jit(solution)/shard_map/all_to_all | solution.py:111
  304.2 192.9 %copy-start.6 = (s32[32,8,16]{2,1,0:T(8,128)}, s32[32,8,16]{2,1,0:T(8,128)S(1)}, u32[]{:S(2)}) copy-start(s32[32,8,16]{2,1,0:T(8,128)S(1)} %copy.60) | copy-start | bytes 49156
  305.2 191.9 %copy-start.7 = (s32[32,8,16]{2,1,0:T(8,128)}, s32[32,8,16]{2,1,0:T(8,128)S(1)}, u32[]{:S(2)}) copy-start(s32[32,8,16]{2,1,0:T(8,128)S(1)} %copy.67) | copy-start | bytes 49156
  503.6 5.3 copy-start.8
  503.6 53.5 %all-to-all-start.3 = ((bf16[32,8,8192]{2,0,1:T(8,128)(2,1)}), bf16[32,8,8192]{2,0,1:T(8,128)(2,1)}, u32[]{:S(2)}, u32[]{:S(2)}) async-start(bf16[32,8,8192]{2,0,1:T(8,128)(2,1)} %copy.53), calls=%async_computation.3 | async-start | bytes 8388608 | tf_op jit(solution)/shard_map/all_to_all | solution.py:104
  571.0 5.6 copy-start.1
  (3 other events, 2.2 us)
Sparse Core Ops, SparseCore 0:
  207.2 283.6 all-reduce.2
where the time goes:
time: 595 us; the launch traced here: 584 us
  waiting for transfers between devices  315 us (53%)
  local copies, waits for them, and re-layouts  110 us (18%)
  starting transfers between devices  73 us (12%)
  matrix products  43.6 us (7%)
  other arithmetic  26.6 us (4%)
  between operations  14.9 us (3%)
    psum x1, waiting for transfers between devices, per_device(): lax.psum((part_hot, part_warm, part_cold), ('wide', 'narrow'))  186 us
    all_to_all x1, waiting for transfers between devices, per_device(): lax.all_to_all(sent_hot, 'wide', split_axis=0, concat_axis=0, tiled=True)  88.8 us
    scatter x3, local copies, waits for them, and re-layouts, pack_rows(): jnp.zeros((devices * capacity, columns), values.dtype).at[placed]  25.4 us
    scatter x3, local copies, waits for them, and re-layouts, pack_rows(): jnp.full((devices * capacity,), -1, jnp.int32).at[placed].set(local_rows)  24.7 us
    dot_general x5, matrix products, one_block(): return jnp.dot(onehot, terms, preferred_element_type=jnp.float32)  13.7 us
    dot_general x8, matrix products, one_block(): lax.dot_general(terms, onehot, (((0,), (0,)), ((), ())), preferred_elemen...  13.6 us
    all_to_all x1, waiting for transfers between devices, per_device(): lax.all_to_all(sent_cold, 'wide', split_axis=0, concat_axis=0, tiled=True)  11.9 us
  transfers between devices with their start and end apart: 13, of which 9 were waited for; matrix products, arithmetic and copies ran while one was open for 24% of the time, Pallas kernels for 0%

commit v1 on v0

v1 whole, which is shorter than its diff:
```python
import math

import jax
import jax.numpy as jnp
from jax import lax
from jax.experimental import pallas as pl
from jax.experimental.pallas import tpu as pltpu
from jax.sharding import PartitionSpec as P

MESH = pl.DeviceIdType.MESH
BF = jnp.bfloat16
F32 = jnp.float32
I32 = jnp.int32

NZ = 8
NP = 32
CAP = 16
LOOK = 2048
HOT = 2
NT = (((1,), (1,)), ((), ()))
TN = (((0,), (0,)), ((), ()))
PIECE = 192


def dot(a, b, dims=(((1,), (0,)), ((), ()))):
    return lax.dot_general(a, b, dims, preferred_element_type=F32)


def iota(shape, dim):
    return lax.broadcasted_iota(I32, shape, dim)


def one(cond):
    return jnp.where(cond, 1.0, 0.0).astype(BF)


def kernel(
    factor,
    own_h, own_w, own_c, loc_h, loc_w, loc_c,
    a_up_w, a_up_c, a_up_h, a_sv_h, a_sv_w, a_sv_c, a_w_w, a_w_c, a_w_h,
    out_th, out_tw, out_tc, out_mh, out_mw, out_mc,
    up_w, up_c, up_h, sv_h, sv_w, sv_c, w_w, w_c, w_h,
    term_w, term_c, term_h,
    tri, ohk, pick, slots, ls, lr, lz, zl,
    s, r, ohh, ring_l, ring_s, got_l, got_s,
    zw, zc, cs, xw, ohw, lows,
    mp, pair, part, zsum, ypart, ysum, xsum, yall, gall,
    in_sem, lab_send, lab_recv, pl_send, pl_recv, z_send, z_recv,
    rl_send, rs_send, rl_recv, rs_recv, ar_send, ar_recv,
):
    wide, narrow = lax.axis_index("wide"), lax.axis_index("narrow")
    me_z, me_y = lax.div(wide, 4), lax.rem(wide, 4)
    me_x, me_c = lax.div(narrow, 2), lax.rem(narrow, 2)
    me_p = me_y * 8 + narrow
    me_j, me_g = lax.rem(me_p, 4), lax.div(me_p, 4)

    def plane_dev(p):
        return (me_z * 4 + lax.div(p, 8), lax.rem(p, 8))

    def z_dev(z):
        return (z * 4 + me_y, narrow)

    def remote(src, dst, ssem, rsem, dev):
        return pltpu.make_async_remote_copy(
            src_ref=src, dst_ref=dst, send_sem=ssem, recv_sem=rsem, device_id=dev, device_id_type=MESH
        )

    def drain(ref, sem):
        pltpu.make_async_copy(ref, ref, sem).wait()

    loads = []
    for n, (src, dst) in enumerate(
        (
            (a_w_w, w_w), (a_up_w, up_w), (a_w_c, w_c), (a_up_c, up_c), (a_up_h, up_h),
            (a_w_h, w_h), (a_sv_h, sv_h), (a_sv_w, sv_w), (a_sv_c, sv_c),
        )
    ):
        copy = pltpu.make_async_copy(src, dst, in_sem.at[n])
        copy.start()
        loads.append(copy)

    barrier = pltpu.get_barrier_semaphore()

    @pl.loop(1, NP)
    def _(i):
        pl.semaphore_signal(barrier, inc=1, device_id=plane_dev(lax.rem(me_p + i, NP)), device_id_type=MESH)

    @pl.loop(1, NZ)
    def _(i):
        pl.semaphore_signal(barrier, inc=1, device_id=z_dev(lax.rem(me_z + i, NZ)), device_id_type=MESH)

    tri[...] = one(iota((256, 256), 0) < iota((256, 256), 1))

    def keys(b, own_ref, loc_ref):
        run = jnp.zeros((256, 1), F32)
        high = jnp.zeros((256, 128), F32)
        low = jnp.zeros((256, 128), F32)
        for k in range(8):
            cols = slice(k * 256, (k + 1) * 256)
            own = own_ref[:, cols]
            key = (own & 31) * 8 + (own >> 5)
            hit = iota((256, 256), 0) == key
            hit_b = one(hit)
            before = dot(hit_b, tri[...]) + run
            place = jnp.sum(jnp.where(hit, before, 0.0), axis=0, keepdims=True).astype(I32)
            run = run + jnp.sum(jnp.where(hit, 1.0, 0.0), axis=1, keepdims=True)
            slots[b, :, cols] = key * CAP + place
            label = loc_ref[:, cols] + 1
            at = iota((128, 256), 0) == place + me_g * CAP
            high += dot(hit_b, jnp.where(at, (label >> 6).astype(F32), 0.0).astype(BF), NT)
            low += dot(hit_b, jnp.where(at, (label & 63).astype(F32), 0.0).astype(BF), NT)
        ls[b] = (high * 64.0 + low).astype(I32).reshape(NP, NZ, 128)

    keys(0, own_w, loc_w)
    keys(1, own_c, loc_c)
    keys(2, own_h, loc_h)

    def project(up, w, term, mask):
        @pl.loop(0, 8)
        def _(i):
            rows = pl.ds(pl.multiple_of(i * 256, 256), 256)
            t = dot(up[rows, :], w[...], NT)
            if mask:
                t = jnp.where(lax.div(iota((256, 128), 1), 32) == me_j, t, 0.0)
            term[rows, :] = t.astype(BF)

    def pack(b, term, first, chunks):
        @pl.loop(0, NP // 2)
        def _(i):
            q = lax.rem(lax.div(me_p, 2) + i, NP // 2)
            for k in range(8):
                cols = slice(k * 256, (k + 1) * 256)
                pick[:, cols] = one(iota((256, 256), 0) + q * 256 == slots[b, :, cols])
            for n in range(chunks):
                res = dot(pick[...], term[:, n * 128:(n + 1) * 128]) if chunks == 1 else None
                if chunks > 1:
                    if n % 2:
                        continue
                    res = dot(pick[...], term[:, n * 128:(n + 2) * 128])
                    s[first + n + 1, pl.ds(q * 2, 2)] = res[:, 128:].astype(BF).reshape(2, NZ, CAP, 128)
                s[first + n, pl.ds(q * 2, 2)] = res[:, :128].astype(BF).reshape(2, NZ, CAP, 128)

    def send_chunk(k):
        pltpu.make_async_copy(s.at[k, me_p], r.at[k, me_p], pl_recv.at[k]).start()

        @pl.loop(1, NP)
        def _(i):
            p = lax.rem(me_p + i, NP)
            remote(s.at[k, p], r.at[k, me_p], pl_send.at[k], pl_recv.at[k], plane_dev(p)).start()

    loads[0].wait()
    loads[1].wait()
    project(up_w, w_w, term_w, False)
    loads[2].wait()
    loads[3].wait()
    project(up_c, w_c, term_c, True)

    pl.semaphore_wait(barrier, NP - 1 + NZ - 1)
    pltpu.make_async_copy(ls.at[:, me_p], lr.at[:, me_p], lab_recv).start()

    @pl.loop(1, NP)
    def _(i):
        p = lax.rem(me_p + i, NP)
        remote(ls.at[:, p], lr.at[:, me_p], lab_send, lab_recv, plane_dev(p)).start()

    pack(0, term_w, 0, 1)
    send_chunk(0)
    pack(1, term_c, 1, 1)
    send_chunk(1)

    def keep(row, value):
        done = 0
        while done < value.shape[0]:
            block, inside = divmod(row + done, PIECE)
            count = min(PIECE - inside, value.shape[0] - done)
            for lane in range(4):
                mp[block // 2, (block % 2) * 4 + lane, inside:inside + count, :] = value[
                    done:done + count, lane * 128:(lane + 1) * 128
                ]
            done += count

    loads[4].wait()
    loads[6].wait()
    loads[7].wait()
    loads[8].wait()
    for m in range(4):
        keep(m * 128, dot(sv_h[:, m * 128:(m + 1) * 128], up_h[...], TN))
    keep(512, dot(sv_w[...], up_w[...], TN))
    keep(640, dot(sv_c[...], up_c[...]))
    keep(672, jnp.zeros((96, 512), F32))
    other = (wide, me_x * 2 + 1 - me_c)
    remote(mp.at[1 - me_c], pair, ar_send.at[0], ar_recv.at[0], other).start()

    loads[5].wait()
    project(up_h, w_h, term_h, False)
    pack(2, term_h, HOT, 4)
    send_chunk(HOT)
    send_chunk(HOT + 1)

    drain(pair, ar_recv.at[0])
    for q in range(NZ):
        part[q] = mp[me_c, q] + pair[q]
    pltpu.make_async_copy(part.at[me_z], zsum.at[me_z], ar_recv.at[1]).start()

    @pl.loop(1, NZ)
    def _(i):
        z = lax.rem(me_z + i, NZ)
        remote(part.at[z], zsum.at[me_z], ar_send.at[1], ar_recv.at[1], z_dev(z)).start()

    drain(lr, lab_recv)
    for b in range(3):
        for j in range(4):
            row = lr[b, j]
            for g in range(1, 8):
                row = row + lr[b, 4 * g + j]
            for z in range(NZ):
                lz[z, b * 4 + j:b * 4 + j + 1, :] = row[z:z + 1, :]

    @pl.loop(0, NZ)
    def _(t):
        for j in range(4):
            ohh[t, :, j * 128:(j + 1) * 128] = one(iota((512, 128), 0) + 1 == lz[t, 8 + j:9 + j, :])

    drain(r.at[0], pl_recv.at[0])
    pltpu.make_async_copy(r.at[0, :, me_z], zw.at[me_z], z_recv.at[0]).start()
    pltpu.make_async_copy(lz.at[me_z, 0:8], zl.at[me_z], z_recv.at[2]).start()

    @pl.loop(1, NZ)
    def _(i):
        t = lax.rem(me_z + i, NZ)
        remote(r.at[0, :, t], zw.at[me_z], z_send.at[0], z_recv.at[0], z_dev(t)).start()
        remote(lz.at[t, 0:8], zl.at[me_z], z_send.at[2], z_recv.at[2], z_dev(t)).start()

    drain(r.at[1], pl_recv.at[1])

    @pl.loop(0, NZ)
    def _(t):
        for g in range(8):
            total = r[1, 4 * g, t].astype(F32)
            for j in range(1, 4):
                total = total + r[1, 4 * g + j, t].astype(F32)
            cs[t, g] = total.astype(BF)

    pltpu.make_async_copy(cs.at[me_z], zc.at[me_z], z_recv.at[1]).start()

    @pl.loop(1, NZ)
    def _(i):
        t = lax.rem(me_z + i, NZ)
        remote(cs.at[t], zc.at[me_z], z_send.at[1], z_recv.at[1], z_dev(t)).start()

    def mix_y():
        drain(zsum, ar_recv.at[1])
        for y in range(4):
            rows = slice(y * 48, (y + 1) * 48)
            total = zsum[0, rows, :]
            for z in range(1, NZ):
                total = total + zsum[z, rows, :]
            ypart[y] = total
        pltpu.make_async_copy(ypart.at[me_y], ysum.at[me_y], ar_recv.at[2]).start()
        for i in range(1, 4):
            y = lax.rem(me_y + i, 4)
            remote(ypart.at[y], ysum.at[me_y], ar_send.at[2], ar_recv.at[2], (me_z * 4 + y, narrow)).start()

    def mix_x():
        drain(ysum, ar_recv.at[2])
        xsum[4] = ysum[0] + ysum[1] + ysum[2] + ysum[3]
        pltpu.make_async_copy(xsum.at[4], xsum.at[me_x], ar_recv.at[3]).start()
        for i in range(1, 4):
            x = lax.rem(me_x + i, 4)
            remote(xsum.at[4], xsum.at[me_x], ar_send.at[3], ar_recv.at[3], (wide, x * 2 + me_c)).start()

    def mix_y_back():
        drain(xsum.at[0:4], ar_recv.at[3])
        yall[4] = (xsum[0] + xsum[1] + xsum[2] + xsum[3]) * factor
        pltpu.make_async_copy(yall.at[4], yall.at[me_y], ar_recv.at[4]).start()
        for i in range(1, 4):
            y = lax.rem(me_y + i, 4)
            remote(yall.at[4], yall.at[me_y], ar_send.at[4], ar_recv.at[4], (me_z * 4 + y, narrow)).start()

    def mix_z_back():
        drain(yall.at[0:4], ar_recv.at[4])
        pltpu.make_async_copy(yall.at[0:4], gall.at[me_c, me_z], ar_recv.at[5]).start()

        @pl.loop(1, NZ)
        def _(i):
            z = lax.rem(me_z + i, NZ)
            remote(yall.at[0:4], gall.at[me_c, me_z], ar_send.at[5], ar_recv.at[5], z_dev(z)).start()

    def mix_pair_back():
        drain(gall.at[0], ar_recv.at[5])
        remote(gall.at[me_c], gall.at[me_c], ar_send.at[6], ar_recv.at[6], other).start()

    def mix_out():
        drain(gall.at[0], ar_recv.at[6])
        for block in range(4):
            for lane in range(4):
                cols = slice(lane * 128, (lane + 1) * 128)
                for y in range(4):
                    value = gall[block // 2, (block % 2) * 4 + lane, y]
                    row = block * PIECE + y * 48
                    for lo, hi, out in ((0, 512, out_mh), (512, 640, out_mw), (640, 672, out_mc)):
                        begin, end = max(row, lo), min(row + 48, hi)
                        if begin < end:
                            out[begin - lo:end - lo, cols] = value[begin - row:end - row]

    def partial(c, t):
        x = jnp.concatenate([r[HOT + c, 4 * g + j, t] for j in range(4) for g in range(8)], axis=0)
        return dot(ohh[t], x)

    def ring(c, step):
        way = 1 - 2 * lax.rem(me_c + c, 2)
        t = lax.rem(me_z + NZ + way * (4 - step), NZ)
        value = partial(c, t)
        if step:
            drain(got_l.at[c, step - 1], rl_recv.at[c, step - 1])
            value = value + got_l[c, step - 1].astype(F32)
        ring_l[c, step] = value.astype(BF)
        if step:
            t = lax.rem(me_z + NZ - way * (4 - step), NZ)
            value = partial(c, t)
            if step > 1:
                drain(got_s.at[c, step - 2], rs_recv.at[c, step - 2])
                value = value + got_s[c, step - 2].astype(F32)
            ring_s[c, step - 1] = value.astype(BF)
        remote(
            ring_l.at[c, step], got_l.at[c, step], rl_send.at[c, step], rl_recv.at[c, step],
            z_dev(lax.rem(me_z + NZ + way, NZ)),
        ).start()
        if step:
            remote(
                ring_s.at[c, step - 1], got_s.at[c, step - 1], rs_send.at[c, step - 1], rs_recv.at[c, step - 1],
                z_dev(lax.rem(me_z + NZ - way, NZ)),
            ).start()

    def ring_end(c):
        value = partial(c, me_z)
        drain(got_l.at[c, 3], rl_recv.at[c, 3])
        drain(got_s.at[c, 2], rs_recv.at[c, 2])
        out_th[:, c * 128:(c + 1) * 128] = value + got_l[c, 3].astype(F32) + got_s[c, 2].astype(F32)

    def arrive(c):
        drain(r.at[HOT + c], pl_recv.at[HOT + c])

    def warm_table():
        drain(zw, z_recv.at[0])
        drain(zl, z_recv.at[2])

        @pl.loop(0, NZ)
        def _(z):
            for j in range(4):
                rows = pl.ds(pl.multiple_of((z * 4 + j) * 128, 128), 128)
                xw[rows, :] = jnp.concatenate([zw[z, 4 * g + j] for g in range(8)], axis=0)

        @pl.loop(0, 8)
        def _(i):
            for z in range(NZ):
                for j in range(4):
                    k = (z * 4 + j) * 128
                    ohw[:, k:k + 128] = one(iota((256, 128), 0) + (i * 256 + 1) == zl[z, j:j + 1, :])
            out_tw[pl.ds(pl.multiple_of(i * 256, 256), 256), :] = dot(ohw[...], xw[...])

    def cold_table():
        drain(zc, z_recv.at[1])
        turned = []
        for j in range(4):
            choose = one(iota((32, 128), 1) == iota((32, 128), 0) + 32 * j)
            turned.append(dot(choose, zc[...].reshape(1024, 128), NT))
            for z in range(NZ):
                k = j * 1024 + z * 128
                lows[:, k:k + 128] = one(iota((128, 128), 0) == ((zl[z, 4 + j:5 + j, :] - 1) & 127))
        for h in range(4):
            for j in range(4):
                for z in range(NZ):
                    k = j * 1024 + z * 128
                    high = (zl[z, 4 + j:5 + j, :] - 1) >> 7
                    for i in range(8):
                        ohw[i * 32:(i + 1) * 32, k:k + 128] = jnp.where(
                            high == h * 8 + i, turned[j][:, z * 128:(z + 1) * 128], 0.0
                        ).astype(BF)
            res = dot(ohw[...], lows[...], NT)
            for i in range(8):
                out_tc[:, (h * 8 + i) * 128:(h * 8 + i + 1) * 128] = res[i * 32:(i + 1) * 32, :]

    arrive(0)
    send_chunk(HOT + 2)
    ring(0, 0)
    mix_y()
    ring(0, 1)
    ring(0, 2)
    mix_x()
    arrive(1)
    send_chunk(HOT + 3)
    ring(1, 0)
    ring(0, 3)
    mix_y_back()
    ring(1, 1)
    ring_end(0)
    ring(1, 2)
    warm_table()
    arrive(2)
    ring(2, 0)
    ring(1, 3)
    mix_z_back()
    ring(2, 1)
    ring_end(1)
    ring(2, 2)
    cold_table()
    arrive(3)
    ring(3, 0)
    ring(2, 3)
    mix_pair_back()
    ring(3, 1)
    ring_end(2)
    ring(3, 2)
    mix_out()
    ring(3, 3)

    for k in range(6):
        drain(r.at[k, 0:NP - 1], pl_send.at[k])
    drain(lr.at[:, 0:NP - 1], lab_send)
    drain(zw.at[0:NZ - 1], z_send.at[0])
    drain(zc.at[0:NZ - 1], z_send.at[1])
    drain(zl.at[0:NZ - 1], z_send.at[2])
    drain(pair, ar_send.at[0])
    drain(zsum.at[0:NZ - 1], ar_send.at[1])
    drain(ysum.at[0:3], ar_send.at[2])
    drain(xsum.at[0:3], ar_send.at[3])
    drain(yall.at[0:3], ar_send.at[4])
    drain(gall.at[0, 0:NZ - 1], ar_send.at[5])
    drain(gall.at[0], ar_send.at[6])
    for c in range(4):
        for step in range(4):
            drain(got_l.at[c, step], rl_send.at[c, step])
        for step in range(3):
            drain(got_s.at[c, step], rs_send.at[c, step])
    ring_end(3)


def per_device(
    upstream_hot, upstream_warm, upstream_cold, saved_hot, saved_warm, saved_cold,
    weight_hot, weight_warm, weight_cold, owner_hot, owner_warm, owner_cold,
    local_hot, local_warm, local_cold,
):
    devices = lax.axis_size("wide") * lax.axis_size("narrow")
    factor = 1.0 / math.sqrt(LOOK * devices)
    rows = [a.reshape(1, LOOK) for a in (owner_hot, owner_warm, owner_cold, local_hot, local_warm, local_cold)]
    anywhere = pl.BlockSpec(memory_space=pl.ANY)
    near = pl.BlockSpec(memory_space=pltpu.VMEM)
    dma = pltpu.SemaphoreType.DMA
    v = pltpu.VMEM

    def body(*refs):
        kernel(factor, *refs)

    return pl.pallas_call(
        body,
        out_shape=(
            jax.ShapeDtypeStruct((512, 512), F32),
            jax.ShapeDtypeStruct((2048, 128), F32),
            jax.ShapeDtypeStruct((32, 4096), F32),
            jax.ShapeDtypeStruct((512, 512), F32),
            jax.ShapeDtypeStruct((128, 512), F32),
            jax.ShapeDtypeStruct((32, 512), F32),
        ),
        in_specs=[near] * 6 + [anywhere] * 9,
        out_specs=(near,) * 6,
        scratch_shapes=[
            v((2048, 512), BF), v((2048, 512), BF), v((2048, 512), BF),
            v((2048, 512), BF), v((2048, 128), BF), v((32, 2048), BF),
            v((128, 512), BF), v((128, 512), BF), v((512, 512), BF),
            v((2048, 128), BF), v((2048, 128), BF), v((2048, 512), BF),
            v((256, 256), BF), v((8, 128), BF), v((256, 2048), BF), v((3, 1, 2048), I32),
            v((3, NP, NZ, 128), I32), v((3, NP, NZ, 128), I32), v((NZ, 16, 128), I32), v((NZ, 8, 128), I32),
            v((6, NP, NZ, CAP, 128), BF), v((6, NP, NZ, CAP, 128), BF), v((NZ, 512, 512), BF),
            v((4, 4, 512, 128), BF), v((4, 3, 512, 128), BF), v((4, 4, 512, 128), BF), v((4, 3, 512, 128), BF),
            v((NZ, NP, CAP, 128), BF), v((NZ, 8, CAP, 128), BF), v((NZ, 8, CAP, 128), BF),
            v((4096, 128), BF), v((256, 4096), BF), v((128, 4096), BF),
            v((2, NZ, PIECE, 128), F32), v((NZ, PIECE, 128), F32), v((NZ, PIECE, 128), F32), v((NZ, PIECE, 128), F32),
            v((4, 48, 128), F32), v((4, 48, 128), F32), v((5, 48, 128), F32), v((5, 48, 128), F32),
            v((2, NZ, 4, 48, 128), F32),
            dma((9,)), dma(()), dma(()), dma((6,)), dma((6,)), dma((3,)), dma((3,)),
            dma((4, 4)), dma((4, 3)), dma((4, 4)), dma((4, 3)), dma((7,)), dma((7,)),
        ],
        compiler_params=pltpu.CompilerParams(
            collective_id=0, has_side_effects=True, vmem_limit_bytes=67_000_000
        ),
    )(
        *rows,
        upstream_warm, upstream_cold, upstream_hot, saved_hot, saved_warm, saved_cold,
        weight_warm, jnp.tile(weight_cold, (4, 1)), weight_hot,
    )


def solution(mesh):
    both = ("wide", "narrow")
    placed = (
        P(both, None), P(both, None), P(both, None), P(both, None), P(both, None), P(None, both),
        P(), P(), P(),
        P(both, None), P(both, None), P(both, None), P(both), P(both), P(both),
    )
    return jax.shard_map(
        per_device,
        mesh=mesh,
        in_specs=placed,
        out_specs=(P(both, None), P(both, None), P(None, both), P(), P(), P()),
        check_vma=False,
    )
```

time: 595 us -> 191 us (0.32); the launches traced: 584 us -> 191 us
  waiting for transfers between devices: 315 us -> 0 us
  Pallas kernels: 0 us -> 182 us
  local copies, waits for them, and re-layouts: 110 us -> 7.89 us
  starting transfers between devices: 73 us -> 0 us
  matrix products: 43.6 us -> 0 us
  other arithmetic: 26.6 us -> 0 us
  between operations: 14.9 us -> 0.66 us
    psum x1 -> x0, waiting for transfers between devices: 186 us -> none  [per_device(): lax.psum((part_hot, part_warm, part_cold), ('wide', 'narrow'))]
    pallas_call x0 -> x1, Pallas kernels: none -> 182 us  [per_device(): pl.pallas_call(body, out_shape=(jax.ShapeDtypeStruct((512, 512), F32), ja...]
    all_to_all x12 -> x0, waiting for transfers between devices: 129 us -> none  [the longest x1 88.8 us: per_device(): lax.all_to_all(sent_hot, 'wide', split_axis=0, concat_axis=0, tiled=True)]
    all_to_all x12 -> x0, starting transfers between devices: 73 us -> none  [the longest x1 11.5 us: per_device(): lax.all_to_all(label_hot, 'wide', split_axis=0, concat_axis=0, tiled=True)]
    scatter x6 -> x0, local copies, waits for them, and re-layouts: 50 us -> none  [the longest x3 25.4 us: pack_rows(): jnp.zeros((devices * capacity, columns), values.dtype).at[placed]]
    dot_general x19 -> x0, matrix products: 43.6 us -> none  [the longest x5 13.7 us: one_block(): return jnp.dot(onehot, terms, preferred_element_type=jnp.float32)]
    reshape x10 -> x0, local copies, waits for them, and re-layouts: 20 us -> none  [the longest x3 10.4 us: pack_rows(): buffer.reshape(wide_size, narrow_size, capacity * columns)]
    all_to_all x11 -> x0, local copies, waits for them, and re-layouts: 16.9 us -> none  [the longest x1 6.45 us: per_device(): lax.all_to_all(sent_hot, 'wide', split_axis=0, concat_axis=0, tiled=True)]
  transfers between devices with their start and end apart: 13 -> 0, of which waited for: 9 -> 0; matrix products, arithmetic and copies ran while one was open for 24% -> 0% of each run, Pallas kernels for 0% -> 0%
where the time goes in v1:
time: 191 us
  Pallas kernels  182 us (95%)
  local copies, waits for them, and re-layouts  7.89 us (4%)
    pallas_call x1, Pallas kernels, per_device(): pl.pallas_call(body, out_shape=(jax.ShapeDtypeStruct((512, 512), F32), ja...  182 us
    unnamed x16, local copies, waits for them, and re-layouts  6.46 us

profile of v1, /device:TPU:2, one launch (start us, length us, event | category | flops | bytes accessed | tf_op | source)
XLA Modules:
  0.0 190.9 jit_solution(6717754741593335527)
XLA Ops:
  0.6 1.4 tile.4
  2.1 182.4 %shard_map.190 = (f32[512,512]{1,0:T(8,128)}, f32[2048,128]{1,0:T(8,128)}, f32[32,4096]{1,0:T(8,128)}, f32[512,512]{1,0:T(8,128)}, f32[128,512]{1,0:T(8,128)}, /*index=5*/f32[32,512]{1,0:T(8,128)}) custom-call(s32[1,2048]{1,0:T(1,128)} %bitcast.8, s32[1,2048]{1,0:T(1,128)} %bitcast.9, s32[1,2048]{1,0:T(1,128)} %bitcast.10, s32[1,2048]{1,0:T(1,128)} %bitcast.11, ...), custom_call_target="tpu_custom_call" | custom-call | tf_op jit(solution)/shard_map/pallas_call | solution.py:455
  184.4 0.0 copy-start.1
  184.5 0.0 copy-start.2
  184.5 2.4 %copy.27 = f32[512,512]{1,0:T(8,128)} copy(f32[512,512]{1,0:T(8,128)} %get-tuple-element.12) | data formatting | bytes 2097152
  186.8 0.0 copy-done.1
  186.8 0.0 copy-start
  186.8 1.0 copy.28
  187.8 0.0 copy-done.2
  187.8 0.0 copy-start.3
  187.8 0.0 copy-start.4
  187.8 0.8 copy.29
  188.6 0.0 copy-done
  188.6 1.0 copy.30
  189.6 0.0 copy-done.3
  189.6 0.7 copy.31
  190.3 0.0 copy-done.4
  190.3 0.6 copy.32
Async XLA Ops:
  184.4 2.4 %copy-start.1 = (f32[2048,128]{1,0:T(8,128)S(1)}, f32[2048,128]{1,0:T(8,128)}, u32[]{:S(2)}) copy-start(f32[2048,128]{1,0:T(8,128)} %get-tuple-element.13) | copy-start | bytes 3145732
  184.5 3.4 %copy-start.2 = (f32[32,4096]{1,0:T(8,128)S(1)}, f32[32,4096]{1,0:T(8,128)}, u32[]{:S(2)}) copy-start(f32[32,4096]{1,0:T(8,128)} %get-tuple-element.14) | copy-start | bytes 1572868
  186.8 1.8 copy-start
  187.8 1.8 copy-start.3
  187.8 2.5 %copy-start.4 = (f32[32,512]{1,0:T(8,128)S(1)}, f32[32,512]{1,0:T(8,128)}, u32[]{:S(2)}) copy-start(f32[32,512]{1,0:T(8,128)} %get-tuple-element.17) | copy-start | bytes 196612

commit v2 on v1

v2 whole, which is shorter than its diff:
```python
import math

import jax
import jax.numpy as jnp
from jax import lax
from jax.experimental import pallas as pl
from jax.experimental.pallas import tpu as pltpu
from jax.sharding import PartitionSpec as P

MESH = pl.DeviceIdType.MESH
BF = jnp.bfloat16
F32 = jnp.float32
I32 = jnp.int32

NZ = 8
NP = 32
CAP = 16
LOOK = 2048
HOT = 1
COLD = 5
NT = (((1,), (1,)), ((), ()))
TN = (((0,), (0,)), ((), ()))
PIECE = 384


def dot(a, b, dims=(((1,), (0,)), ((), ()))):
    return lax.dot_general(a, b, dims, preferred_element_type=F32)


def iota(shape, dim):
    return lax.broadcasted_iota(I32, shape, dim)


def one(cond):
    return jnp.where(cond, 1.0, 0.0).astype(BF)


def kernel(
    factor,
    own_h, own_w, own_c, loc_h, loc_w, loc_c,
    a_up_w, a_up_c, a_up_h, a_sv_h, a_sv_w, a_sv_c, a_w_w, a_w_c, a_w_h,
    hbm_th, hbm_tw, hbm_tc, hbm_mh, hbm_mw, hbm_mc,
    out_th, out_tw, out_tc, out_mh, out_mw, out_mc,
    up_w, up_c, up_h, sv_h, sv_w, sv_c, w_w, w_c, w_h,
    term_w, term_c, term_h,
    tri, pick, slots, ls, lr, lz, zl,
    s, r, s_c, r_c, ohh, ring_l, ring_s, got_l, got_s,
    zw, zc, cs, xw, ohw, lows,
    mp, pair, part, bsum, bpart, ssum, spart, zsum, total, sall, gall,
    in_sem, out_sem, lab_send, lab_recv, pl_send, pl_recv, z_send, z_recv,
    rl_send, rs_send, rl_recv, rs_recv, ar_send, ar_recv,
):
    wide, narrow = lax.axis_index("wide"), lax.axis_index("narrow")
    me_z, me_y = lax.div(wide, 4), lax.rem(wide, 4)
    me_x, me_c = lax.div(narrow, 2), lax.rem(narrow, 2)
    me_p = me_y * 8 + narrow
    other = (wide, me_x * 2 + 1 - me_c)

    def plane_dev(p):
        return (me_z * 4 + lax.div(p, 8), lax.rem(p, 8))

    def z_dev(z):
        return (z * 4 + me_y, narrow)

    def chip(i):
        x, y = me_x + lax.rem(i, 4), me_y + i + lax.div(i, 4)
        return lax.rem(y, 4) * 4 + lax.rem(x, 4)

    def to_peers(send):
        send(me_p + 1 - 2 * me_c)

        @pl.loop(1, NP // 2)
        def _(i):
            send(chip(i) * 2)
            send(chip(i) * 2 + 1)

    def remote(src, dst, ssem, rsem, dev):
        return pltpu.make_async_remote_copy(
            src_ref=src, dst_ref=dst, send_sem=ssem, recv_sem=rsem, device_id=dev, device_id_type=MESH
        )

    def drain(ref, sem):
        pltpu.make_async_copy(ref, ref, sem).wait()

    loads = {}
    for n, (name, src, dst) in enumerate(
        (
            ("w_w", a_w_w, w_w), ("up_w", a_up_w, up_w), ("up_h", a_up_h, up_h), ("sv_h", a_sv_h, sv_h),
            ("sv_w", a_sv_w, sv_w), ("up_c", a_up_c, up_c), ("sv_c", a_sv_c, sv_c), ("w_h", a_w_h, w_h),
            ("w_c", a_w_c, w_c),
        )
    ):
        loads[name] = pltpu.make_async_copy(src, dst, in_sem.at[n])
        loads[name].start()

    barrier = pltpu.get_barrier_semaphore()

    @pl.loop(1, NP)
    def _(i):
        pl.semaphore_signal(barrier, inc=1, device_id=plane_dev(lax.rem(me_p + i, NP)), device_id_type=MESH)

    @pl.loop(1, NZ)
    def _(i):
        pl.semaphore_signal(barrier, inc=1, device_id=z_dev(lax.rem(me_z + i, NZ)), device_id_type=MESH)

    def exact(values):
        return values.astype(F32).astype(BF)

    def match(row, rows=256):
        return jnp.where(exact(iota((rows, row.shape[1]), 0)) == row, jnp.ones((), BF), jnp.zeros((), BF))

    def near(row, base):
        return exact(jnp.clip(row - base, -1, 256))

    def keys(b, own_ref, loc_ref):
        own, label = own_ref[...], loc_ref[...] + 1
        key = exact((own & 31) * 8 + (own >> 5))
        if b < 2:
            base = ((own & 31) * 8 + (own >> 5)) * CAP
        else:
            base = (own & 31) * 128 + (((own >> 5) + me_p) & 7) * CAP
        high, low = exact(label >> 6), exact(label & 63)
        lane = exact(iota((128, 256), 0) & 15)
        none = jnp.zeros((), BF)
        run = jnp.zeros((256, 128), F32)
        both = jnp.zeros((256, 256), F32)
        for k in range(8):
            cols = slice(k * 256, (k + 1) * 256)
            hit = match(key[:, cols])
            count = dot(hit, tri[...])
            before = count[:, 0:256] + jnp.concatenate([run, run], axis=1)
            run = run + count[:, 256:384]
            place = jnp.sum(before * hit.astype(F32), axis=0, keepdims=True)
            slots[b, :, cols] = base[:, cols] + place.astype(I32)
            at = lane == place.astype(BF)
            parts = [jnp.where(at, high[:, cols], none), jnp.where(at, low[:, cols], none)]
            both += dot(hit, jnp.concatenate(parts, axis=0), NT)
        found = both[:, 0:128] * 64.0 + both[:, 128:]
        block = ((iota((256, 128), 0) & 7) + me_p) & 7
        found = jnp.where((iota((256, 128), 1) >> 4) == block, found, 0.0)
        ls[b] = jnp.sum(found.reshape(NP, NZ, 128), axis=1, keepdims=True).astype(I32)

    def project(up, w, term):
        @pl.loop(0, 2)
        def _(i):
            rows = pl.ds(pl.multiple_of(i * 1024, 1024), 1024)
            term[rows, :] = dot(up[rows, :], w[...], NT).astype(BF)

    def send_one(k, p):
        remote(s.at[k, p], r.at[k, me_p], pl_send.at[k], pl_recv.at[k], plane_dev(p)).start()

    def picks(b, q):
        for k in range(8):
            cols = slice(k * 256, (k + 1) * 256)
            pick[:, cols] = match(near(slots[b, :, cols], q * 256))

    def pack(b, term, first, chunks, extra=None):
        @pl.loop(0, NP // 2)
        def _(i):
            q = chip(i)
            picks(b, q)
            for n in range(0, chunks, 2):
                width = min(2, chunks - n)
                if width == 1:
                    res = dot(pick[:, :1024], term[:1024]) + dot(pick[:, 1024:], term[1024:])
                else:
                    res = dot(pick[...], term[:, n * 128:(n + width) * 128])
                res = res.astype(BF)
                for m in range(width):
                    s[first + n + m, pl.ds(q * 2, 2)] = res[:, m * 128:(m + 1) * 128].reshape(2, NZ, CAP, 128)

            @pl.when(i > 1)
            def _():
                last = chip(i - 1)
                send_one(first, last * 2)
                send_one(first, last * 2 + 1)

            if extra is not None:
                pl.when(i == 5)(extra)

        final = chip(NP // 2 - 1)
        pltpu.make_async_copy(s.at[first, me_p], r.at[first, me_p], pl_recv.at[first]).start()
        send_one(first, me_p + 1 - 2 * me_c)
        send_one(first, final * 2)
        send_one(first, final * 2 + 1)

    def pack_cold(part):
        if part == 0:
            loads["w_c"].wait()
            term_c[...] = dot(w_c[...], up_c[...], NT).astype(BF)

        @pl.loop(part * 4, part * 4 + 4)
        def _(i):
            q = chip(i)
            picks(2, q)
            res = dot(term_c[...], pick[...], NT).astype(BF)
            s_c[q * 2] = res[:, :128]
            s_c[q * 2 + 1] = res[:, 128:]

    def send_cold():
        pltpu.make_async_copy(s_c.at[me_p], r_c.at[me_p], pl_recv.at[COLD]).start()

        to_peers(
            lambda p: remote(
                s_c.at[p], r_c.at[me_p], pl_send.at[COLD], pl_recv.at[COLD], plane_dev(p)
            ).start()
        )

    def send_chunk(k):
        pltpu.make_async_copy(s.at[k, me_p], r.at[k, me_p], pl_recv.at[k]).start()

        to_peers(lambda p: send_one(k, p))

    def send_labels(n, lo, hi):
        pltpu.make_async_copy(ls.at[lo:hi, me_p], lr.at[lo:hi, me_p], lab_recv.at[n]).start()

        to_peers(
            lambda p: remote(
                ls.at[lo:hi, p], lr.at[lo:hi, me_p], lab_send.at[n], lab_recv.at[n], plane_dev(p)
            ).start()
        )

    def keep(row, value):
        done = 0
        while done < value.shape[0]:
            half, inside = divmod(row + done, PIECE)
            count = min(PIECE - inside, value.shape[0] - done)
            for lane in range(4):
                mp[half, lane, inside:inside + count, :] = value[done:done + count, lane * 128:(lane + 1) * 128]
            done += count

    def mix_terms():
        for name in ("up_h", "sv_h", "sv_w", "up_c", "sv_c"):
            loads[name].wait()
        for m in range(4):
            keep(m * 128, dot(sv_h[:, m * 128:(m + 1) * 128], up_h[...], TN))
        keep(512, dot(sv_w[...], up_w[...], TN))
        keep(640, dot(sv_c[...], up_c[...]))
        keep(672, jnp.zeros((96, 512), F32))

    def mix_pair():
        remote(mp.at[1 - me_c], pair, ar_send.at[0], ar_recv.at[0], other).start()

    me_a = me_x + me_c * (me_y - me_x)
    me_b = me_y + me_c * (me_x - me_y)

    def a_dev(k):
        return (me_z * 4 + me_y + me_c * (k - me_y), (k + me_c * (me_x - k)) * 2 + me_c)

    def b_dev(k):
        return (me_z * 4 + k + me_c * (me_y - k), (me_x + me_c * (k - me_x)) * 2 + me_c)

    def spread(n, src_of, dst, dev, me, count):
        pltpu.make_async_copy(src_of(me), dst, ar_recv.at[n]).start()

        @pl.loop(1, count)
        def _(i):
            k = lax.rem(me + i, count)
            remote(src_of(k), dst, ar_send.at[n], ar_recv.at[n], dev(k)).start()

    def mix_big():
        drain(pair, ar_recv.at[0])
        for k in range(4):
            part[k] = mp[me_c, k] + pair[k]
        spread(1, lambda k: part.at[k], bsum.at[me_a], a_dev, me_a, 4)

    def mix_small():
        drain(bsum, ar_recv.at[1])
        for k in range(4):
            rows = slice(k * 96, (k + 1) * 96)
            bpart[k] = bsum[0, rows] + bsum[1, rows] + bsum[2, rows] + bsum[3, rows]
        spread(2, lambda k: bpart.at[k], ssum.at[me_b], b_dev, me_b, 4)

    def mix_z():
        drain(ssum, ar_recv.at[2])
        spart[...] = (ssum[0] + ssum[1] + ssum[2] + ssum[3]).astype(BF)
        spread(3, lambda k: spart, zsum.at[me_z], z_dev, me_z, NZ)

    def mix_small_back():
        drain(zsum, ar_recv.at[3])
        added = zsum[0].astype(F32)
        for z in range(1, NZ):
            added = added + zsum[z].astype(F32)
        total[...] = added * factor
        spread(4, lambda k: total, sall.at[me_b], b_dev, me_b, 4)

    def mix_big_back():
        drain(sall, ar_recv.at[4])
        spread(5, lambda k: sall, gall.at[me_c, me_a], a_dev, me_a, 4)

    def mix_pair_back():
        drain(gall.at[0], ar_recv.at[5])
        remote(gall.at[me_c], gall.at[me_c], ar_send.at[6], ar_recv.at[6], other).start()

    def mix_out():
        drain(gall.at[0], ar_recv.at[6])
        for half in range(2):
            for lane in range(4):
                cols = slice(lane * 128, (lane + 1) * 128)
                for b in range(4):
                    value = gall[half, lane, b]
                    row = half * PIECE + b * 96
                    for lo, hi, out in ((0, 512, out_mh), (512, 640, out_mw), (640, 672, out_mc)):
                        begin, end = max(row, lo), min(row + 96, hi)
                        if begin < end:
                            out[begin - lo:end - lo, cols] = value[begin - row:end - row]

    def sort_labels(b):
        lz[b] = jnp.zeros((NZ, 8, 128), I32)
        block, z_at = iota((NZ, 128), 1) >> 4, iota((NZ, 128), 0)
        for j in range(4):
            row = jnp.zeros((NZ, 128), I32)
            for p in range(8):
                row = row + jnp.where(block == ((z_at + p) & 7), lr[b, 8 * j + p], 0)
            for z in range(NZ):
                lz[b, z, j:j + 1, :] = row[z:z + 1, :]

    def hot_rows():
        @pl.loop(0, NZ)
        def _(t):
            for j in range(4):
                row = lz[1, t, j:j + 1, :] - 1
                for half in range(2):
                    ohh[t, half * 256:(half + 1) * 256, j * 128:(j + 1) * 128] = match(near(row, half * 256))

    def labels_on(b, n):
        spread_z(lambda t: lz.at[b, t], zl.at[n, me_z], z_send.at[2 + n], z_recv.at[2 + n])

    def spread_z(src_of, dst, ssem, rsem):
        pltpu.make_async_copy(src_of(me_z), dst, rsem).start()

        @pl.loop(1, NZ)
        def _(i):
            t = lax.rem(me_z + i, NZ)
            remote(src_of(t), dst, ssem, rsem, z_dev(t)).start()

    def warm_on():
        drain(r.at[0], pl_recv.at[0])
        spread_z(lambda t: r.at[0, :, t], zw.at[me_z], z_send.at[0], z_recv.at[0])

    def cold_on():
        drain(r_c, pl_recv.at[COLD])

        @pl.loop(0, NZ)
        def _(t):
            for j in range(4):
                parts = [
                    jnp.where((iota((32, 128), 1) >> 4) == ((t + p) & 7), r_c[8 * j + p].astype(F32), 0.0)
                    for p in range(8)
                ]
                cs[t, :, j * 128:(j + 1) * 128] = sum(parts).astype(BF)

        spread_z(lambda t: cs.at[t], zc.at[me_z], z_send.at[1], z_recv.at[1])

    def leave(n, src, dst):
        copy = pltpu.make_async_copy(src, dst, out_sem.at[n])
        copy.start()
        leaving.append(copy)

    leaving = []

    def partial(c, t):
        x = jnp.concatenate(
            [r[HOT + c, 8 * j + lax.rem(i + NZ - t, NZ), t] for j in range(4) for i in range(8)], axis=0
        )
        return dot(ohh[t], x)

    def ring(c, step):
        way = 1 - 2 * lax.rem(me_c + c, 2)
        value = partial(c, lax.rem(me_z + NZ + way * (4 - step), NZ))
        if step:
            drain(got_l.at[c, step - 1], rl_recv.at[c, step - 1])
            value = value + got_l[c, step - 1].astype(F32)
        ring_l[c, step] = value.astype(BF)
        if step:
            value = partial(c, lax.rem(me_z + NZ - way * (4 - step), NZ))
            if step > 1:
                drain(got_s.at[c, step - 2], rs_recv.at[c, step - 2])
                value = value + got_s[c, step - 2].astype(F32)
            ring_s[c, step - 1] = value.astype(BF)
        remote(
            ring_l.at[c, step], got_l.at[c, step], rl_send.at[c, step], rl_recv.at[c, step],
            z_dev(lax.rem(me_z + NZ + way, NZ)),
        ).start()
        if step:
            remote(
                ring_s.at[c, step - 1], got_s.at[c, step - 1], rs_send.at[c, step - 1], rs_recv.at[c, step - 1],
                z_dev(lax.rem(me_z + NZ - way, NZ)),
            ).start()

    def ring_end(c):
        value = partial(c, me_z)
        drain(got_l.at[c, 3], rl_recv.at[c, 3])
        drain(got_s.at[c, 2], rs_recv.at[c, 2])
        cols = slice(c * 128, (c + 1) * 128)
        out_th[:, cols] = value + got_l[c, 3].astype(F32) + got_s[c, 2].astype(F32)
        leave(c, out_th.at[:, cols], hbm_th.at[:, cols])

    def arrive(c):
        drain(r.at[HOT + c], pl_recv.at[HOT + c])

    def warm_table(half):
        if half == 0:
            drain(zw, z_recv.at[0])
            drain(zl.at[0], z_recv.at[2])

            @pl.loop(0, NZ)
            def _(z):
                for j in range(4):
                    rows = pl.ds(pl.multiple_of((z * 4 + j) * 128, 128), 128)
                    xw[rows, :] = jnp.concatenate(
                        [zw[z, 8 * j + lax.rem(i + NZ - me_z, NZ)] for i in range(8)], axis=0
                    )

        @pl.loop(half * 4, half * 4 + 4)
        def _(i):
            for z in range(NZ):
                for j in range(4):
                    k = (z * 4 + j) * 128
                    ohw[:, k:k + 128] = match(near(zl[0, z, j:j + 1, :] - 1, i * 256))
            res = dot(ohw[:, :2048], xw[:2048]) + dot(ohw[:, 2048:], xw[2048:])
            out_tw[pl.ds(pl.multiple_of(i * 256, 256), 256), :] = res

        if half:
            leave(4, out_tw, hbm_tw)

    def cold_table():
        drain(zc, z_recv.at[1])
        drain(zl.at[1], z_recv.at[3])
        for z in range(NZ):
            for j in range(4):
                k = (z * 4 + j) * 128
                lows[:, k:k + 128] = match(exact((zl[1, z, j:j + 1, :] - 1) & 127), 128)

        @pl.loop(0, 4)
        def _(h):
            for z in range(NZ):
                for j in range(4):
                    k = (z * 4 + j) * 128
                    high = near((zl[1, z, j:j + 1, :] - 1) >> 7, h * 8)
                    for i in range(8):
                        here = jnp.broadcast_to(high, (32, 128)) == jnp.full((), i, BF)
                        ohw[i * 32:(i + 1) * 32, k:k + 128] = jnp.where(
                            here, zc[z, :, j * 128:(j + 1) * 128], jnp.zeros((), BF)
                        )
            res = dot(ohw[:, :2048], lows[:, :2048], NT) + dot(ohw[:, 2048:], lows[:, 2048:], NT)
            for i in range(8):
                out_tc[:, pl.ds(pl.multiple_of(h * 1024 + i * 128, 128), 128)] = res[i * 32:(i + 1) * 32, :]

        leave(5, out_tc, hbm_tc)

    tri[:, 0:256] = one(iota((256, 256), 0) < iota((256, 256), 1))
    tri[:, 256:384] = jnp.ones((256, 128), BF)
    keys(0, own_w, loc_w)
    loads["w_w"].wait()
    loads["up_w"].wait()
    project(up_w, w_w, term_w)
    mix_terms()
    pl.semaphore_wait(barrier, NP - 1 + NZ - 1)
    mix_pair()
    pack(0, term_w, 0, 1)
    keys(1, own_h, loc_h)
    send_labels(0, 0, 2)
    loads["w_h"].wait()
    project(up_h, w_h, term_h)
    mix_big()
    pack(1, term_h, HOT, 4, warm_on)
    mix_small()
    send_chunk(HOT + 1)
    drain(lr.at[0:2], lab_recv.at[0])
    sort_labels(0)
    labels_on(0, 0)
    sort_labels(1)
    hot_rows()
    keys(2, own_c, loc_c)
    pack_cold(0)
    arrive(0)
    ring(0, 0)
    send_chunk(HOT + 2)
    send_labels(1, 2, 3)
    pack_cold(1)
    ring(0, 1)
    pack_cold(2)
    pack_cold(3)
    ring(0, 2)
    mix_z()
    arrive(1)
    ring(1, 0)
    send_chunk(HOT + 3)
    ring(0, 3)
    ring(1, 1)
    ring(1, 2)
    mix_small_back()
    arrive(2)
    ring(2, 0)
    send_cold()
    ring(1, 3)
    ring(2, 1)
    warm_table(0)
    ring(2, 2)
    mix_big_back()
    ring_end(0)
    arrive(3)
    ring(3, 0)
    ring(2, 3)
    drain(lr.at[2], lab_recv.at[1])
    sort_labels(2)
    labels_on(2, 1)
    ring(3, 1)
    warm_table(1)
    ring(3, 2)
    mix_pair_back()
    cold_on()
    ring(3, 3)
    ring_end(1)
    ring_end(2)
    mix_out()
    leave(6, out_mh, hbm_mh)
    leave(7, out_mw, hbm_mw)
    leave(8, out_mc, hbm_mc)
    cold_table()

    for k in range(5):
        drain(r.at[k, 0:NP - 1], pl_send.at[k])
    drain(r_c.at[0:NP - 1], pl_send.at[COLD])
    drain(lr.at[0:2, 0:NP - 1], lab_send.at[0])
    drain(lr.at[2, 0:NP - 1], lab_send.at[1])
    drain(zw.at[0:NZ - 1], z_send.at[0])
    drain(zc.at[0:NZ - 1], z_send.at[1])
    drain(zl.at[0, 0:NZ - 1], z_send.at[2])
    drain(zl.at[1, 0:NZ - 1], z_send.at[3])
    drain(pair, ar_send.at[0])
    drain(bsum.at[0:3], ar_send.at[1])
    drain(ssum.at[0:3], ar_send.at[2])
    drain(zsum.at[0:NZ - 1], ar_send.at[3])
    drain(sall.at[0:3], ar_send.at[4])
    drain(gall.at[0, 0:3], ar_send.at[5])
    drain(gall.at[0], ar_send.at[6])
    for c in range(4):
        for step in range(4):
            drain(got_l.at[c, step], rl_send.at[c, step])
        for step in range(3):
            drain(got_s.at[c, step], rs_send.at[c, step])
    ring_end(3)
    for copy in leaving:
        copy.wait()


def write_out(*refs):
    ins, outs, rooms, (sem,) = refs[:6], refs[6:12], refs[12:18], refs[18:]
    copies = []
    n = 0
    for src, room, dst in zip(ins, rooms, outs):
        cuts = 4 if src.shape[0] >= 256 else 1
        rows = src.shape[0] // cuts
        for k in range(cuts):
            here = pl.ds(k * rows, rows)
            first = pltpu.make_async_copy(src.at[here], room.at[here], sem.at[n])
            second = pltpu.make_async_copy(room.at[here], dst.at[here], sem.at[n + 1])
            first.start()
            copies.append((first, second))
            n += 2
    for first, second in copies:
        first.wait()
        second.start()
    for _, second in copies:
        second.wait()


def per_device(
    upstream_hot, upstream_warm, upstream_cold, saved_hot, saved_warm, saved_cold,
    weight_hot, weight_warm, weight_cold, owner_hot, owner_warm, owner_cold,
    local_hot, local_warm, local_cold,
):
    devices = lax.axis_size("wide") * lax.axis_size("narrow")
    factor = 1.0 / math.sqrt(LOOK * devices)
    rows = [a.reshape(1, LOOK) for a in (owner_hot, owner_warm, owner_cold, local_hot, local_warm, local_cold)]
    anywhere = pl.BlockSpec(memory_space=pl.ANY)
    near = pl.BlockSpec(memory_space=pltpu.VMEM)
    dma = pltpu.SemaphoreType.DMA
    v = pltpu.VMEM
    results = tuple(
        jax.ShapeDtypeStruct(shape, F32)
        for shape in ((512, 512), (2048, 128), (32, 4096), (512, 512), (128, 512), (32, 512))
    )

    def body(*refs):
        kernel(factor, *refs)

    found = pl.pallas_call(
        body,
        out_shape=results,
        in_specs=[near] * 6 + [anywhere] * 9,
        out_specs=(anywhere,) * 6,
        scratch_shapes=[
            *(v(a.shape, F32) for a in results),
            v((2048, 512), BF), v((2048, 512), BF), v((2048, 512), BF),
            v((2048, 512), BF), v((2048, 128), BF), v((32, 2048), BF),
            v((128, 512), BF), v((32, 512), BF), v((512, 512), BF),
            v((2048, 128), BF), v((32, 2048), BF), v((2048, 512), BF),
            v((256, 384), BF), v((256, 2048), BF), v((3, 1, 2048), I32),
            v((3, NP, 1, 128), I32), v((3, NP, 1, 128), I32), v((3, NZ, 8, 128), I32), v((2, NZ, 8, 128), I32),
            v((5, NP, NZ, CAP, 128), BF), v((5, NP, NZ, CAP, 128), BF), v((NP, 32, 128), BF), v((NP, 32, 128), BF),
            v((NZ, 512, 512), BF),
            v((4, 4, 512, 128), BF), v((4, 3, 512, 128), BF), v((4, 4, 512, 128), BF), v((4, 3, 512, 128), BF),
            v((NZ, NP, CAP, 128), BF), v((NZ, 32, 512), BF), v((NZ, 32, 512), BF),
            v((4096, 128), BF), v((256, 4096), BF), v((128, 4096), BF),
            v((2, 4, PIECE, 128), F32), v((4, PIECE, 128), F32), v((4, PIECE, 128), F32), v((4, PIECE, 128), F32),
            v((4, 96, 128), F32), v((4, 96, 128), F32), v((96, 128), BF), v((NZ, 96, 128), BF), v((96, 128), F32),
            v((4, 96, 128), F32), v((2, 4, 4, 96, 128), F32),
            dma((9,)), dma((9,)), dma((2,)), dma((2,)), dma((6,)), dma((6,)), dma((4,)), dma((4,)),
            dma((4, 4)), dma((4, 3)), dma((4, 4)), dma((4, 3)), dma((7,)), dma((7,)),
        ],
        compiler_params=pltpu.CompilerParams(
            collective_id=0, has_side_effects=True, vmem_limit_bytes=67_000_000
        ),
    )(
        *rows,
        upstream_warm, upstream_cold, upstream_hot, saved_hot, saved_warm, saved_cold,
        weight_warm, weight_cold, weight_hot,
    )
    return pl.pallas_call(
        write_out,
        out_shape=results,
        in_specs=[anywhere] * 6,
        out_specs=(anywhere,) * 6,
        scratch_shapes=[v(a.shape, F32) for a in results] + [dma((36,))],
    )(*found)


def solution(mesh):
    both = ("wide", "narrow")
    placed = (
        P(both, None), P(both, None), P(both, None), P(both, None), P(both, None), P(None, both),
        P(), P(), P(),
        P(both, None), P(both, None), P(both, None), P(both), P(both), P(both),
    )
    return jax.shard_map(
        per_device,
        mesh=mesh,
        in_specs=placed,
        out_specs=(P(both, None), P(both, None), P(None, both), P(), P(), P()),
        check_vma=False,
    )
```

time: 191 us -> 130 us (0.68)
  Pallas kernels: 182 us -> 129 us
  local copies, waits for them, and re-layouts: 7.89 us -> 0 us
    pallas_call x1 -> x2, Pallas kernels: 182 us -> 129 us  [the longest x1 125 us: per_device(): pl.pallas_call(body, out_shape=results, in_specs=[near] * 6 + [anywhere]...]
    unnamed x16 -> x0, local copies, waits for them, and re-layouts: 6.46 us -> none
where the time goes in v2:
time: 130 us
  Pallas kernels  129 us (99%)
    pallas_call x1, Pallas kernels, per_device(): pl.pallas_call(body, out_shape=results, in_specs=[near] * 6 + [anywhere]...  125 us
    pallas_call x1, Pallas kernels, per_device(): pl.pallas_call(write_out, out_shape=results, in_specs=[anywhere] * 6, out...  3.61 us

profile of v2, /device:TPU:2, one launch (start us, length us, event | category | flops | bytes accessed | tf_op | source)
XLA Modules:
  0.0 129.8 jit_solution(14357596029619433085)
XLA Ops:
  0.6 125.4 %shard_map.190 = (f32[512,512]{1,0:T(8,128)}, f32[2048,128]{1,0:T(8,128)}, f32[32,4096]{1,0:T(8,128)}, f32[512,512]{1,0:T(8,128)}, f32[128,512]{1,0:T(8,128)}, /*index=5*/f32[32,512]{1,0:T(8,128)}) custom-call(s32[1,2048]{1,0:T(1,128)} %bitcast.6, s32[1,2048]{1,0:T(1,128)} %bitcast.7, s32[1,2048]{1,0:T(1,128)} %bitcast.8, s32[1,2048]{1,0:T(1,128)} %bitcast.9, ...), custom_call_target="tpu_custom_call" | custom-call | tf_op jit(solution)/shard_map/pallas_call | solution.py:590
  126.0 3.6 %shard_map.191 = (f32[512,512]{1,0:T(8,128)}, f32[2048,128]{1,0:T(8,128)}, f32[32,4096]{1,0:T(8,128)}, f32[512,512]{1,0:T(8,128)}, f32[128,512]{1,0:T(8,128)}, /*index=5*/f32[32,512]{1,0:T(8,128)}) custom-call(f32[512,512]{1,0:T(8,128)} %get-tuple-element.12.refs_0_, f32[2048,128]{1,0:T(8,128)} %get-tuple-element.13.refs_1_, ...), custom_call_target="tpu_custom_call" | custom-call | tf_op jit(solution)/shard_map/pallas_call | solution.py:622

commit v3 on v2

--- a/solution.py
+++ b/solution.py
@@ -46,7 +46,7 @@
     tri, pick, slots, ls, lr, lz, zl,
     s, r, s_c, r_c, ohh, ring_l, ring_s, got_l, got_s,
     zw, zc, cs, xw, ohw, lows,
-    mp, pair, part, bsum, bpart, ssum, spart, zsum, total, sall, gall,
+    mp, pair, part, zsum, apart, asum, bpart, bsum, total, zall, gall,
     in_sem, out_sem, lab_send, lab_recv, pl_send, pl_recv, z_send, z_recv,
     rl_send, rs_send, rl_recv, rs_recv, ar_send, ar_recv,
 ):
@@ -65,6 +65,9 @@
     def chip(i):
         x, y = me_x + lax.rem(i, 4), me_y + i + lax.div(i, 4)
         return lax.rem(y, 4) * 4 + lax.rem(x, 4)
+
+    def at(z):
+        return lax.rem(z + 2 * NZ - me_z - 3, NZ)
 
     def to_peers(send):
         send(me_p + 1 - 2 * me_c)
@@ -116,7 +119,7 @@
         own, label = own_ref[...], loc_ref[...] + 1
         key = exact((own & 31) * 8 + (own >> 5))
         if b < 2:
-            base = ((own & 31) * 8 + (own >> 5)) * CAP
+            base = ((own & 31) * 8 + (((own >> 5) + (13 - me_z)) & 7)) * CAP
         else:
             base = (own & 31) * 128 + (((own >> 5) + me_p) & 7) * CAP
         high, low = exact(label >> 6), exact(label & 63)
@@ -132,8 +135,8 @@
             run = run + count[:, 256:384]
             place = jnp.sum(before * hit.astype(F32), axis=0, keepdims=True)
             slots[b, :, cols] = base[:, cols] + place.astype(I32)
-            at = lane == place.astype(BF)
-            parts = [jnp.where(at, high[:, cols], none), jnp.where(at, low[:, cols], none)]
+            there = lane == place.astype(BF)
+            parts = [jnp.where(there, high[:, cols], none), jnp.where(there, low[:, cols], none)]
             both += dot(hit, jnp.concatenate(parts, axis=0), NT)
         found = both[:, 0:128] * 64.0 + both[:, 128:]
         block = ((iota((256, 128), 0) & 7) + me_p) & 7
@@ -154,7 +157,7 @@
             cols = slice(k * 256, (k + 1) * 256)
             pick[:, cols] = match(near(slots[b, :, cols], q * 256))
 
-    def pack(b, term, first, chunks, extra=None):
+    def pack(b, term, first, chunks, extra, when):
         @pl.loop(0, NP // 2)
         def _(i):
             q = chip(i)
@@ -175,8 +178,7 @@
                 send_one(first, last * 2)
                 send_one(first, last * 2 + 1)
 
-            if extra is not None:
-                pl.when(i == 5)(extra)
+            pl.when(i == when)(extra)
 
         final = chip(NP // 2 - 1)
         pltpu.make_async_copy(s.at[first, me_p], r.at[first, me_p], pl_recv.at[first]).start()
@@ -211,6 +213,14 @@
 
         to_peers(lambda p: send_one(k, p))
 
+    def send_part(k, n, lo, hi):
+        pltpu.make_async_copy(s.at[k, me_p, lo:hi], r.at[k, me_p, lo:hi], pl_recv.at[n]).start()
+        to_peers(
+            lambda p: remote(
+                s.at[k, p, lo:hi], r.at[k, me_p, lo:hi], pl_send.at[n], pl_recv.at[n], plane_dev(p)
+            ).start()
+        )
+
     def send_labels(n, lo, hi):
         pltpu.make_async_copy(ls.at[lo:hi, me_p], lr.at[lo:hi, me_p], lab_recv.at[n]).start()
 
@@ -224,9 +234,12 @@
         done = 0
         while done < value.shape[0]:
             half, inside = divmod(row + done, PIECE)
-            count = min(PIECE - inside, value.shape[0] - done)
+            upper, inside = divmod(inside, PIECE // 2)
+            count = min(PIECE // 2 - inside, value.shape[0] - done)
             for lane in range(4):
-                mp[half, lane, inside:inside + count, :] = value[done:done + count, lane * 128:(lane + 1) * 128]
+                mp[half, upper * 4 + lane, inside:inside + count, :] = value[
+                    done:done + count, lane * 128:(lane + 1) * 128
+                ]
             done += count
 
     def mix_terms():
@@ -258,35 +271,32 @@
             k = lax.rem(me + i, count)
             remote(src_of(k), dst, ar_send.at[n], ar_recv.at[n], dev(k)).start()
 
-    def mix_big():
+    def mix_z():
         drain(pair, ar_recv.at[0])
+        for q in range(NZ):
+            part[q] = (mp[me_c, q] + pair[q]).astype(BF)
+        spread(1, lambda k: part.at[k], zsum.at[me_z], z_dev, me_z, NZ)
+
+    def mix_a():
+        drain(zsum, ar_recv.at[1])
         for k in range(4):
-            part[k] = mp[me_c, k] + pair[k]
-        spread(1, lambda k: part.at[k], bsum.at[me_a], a_dev, me_a, 4)
-
-    def mix_small():
-        drain(bsum, ar_recv.at[1])
-        for k in range(4):
-            rows = slice(k * 96, (k + 1) * 96)
-            bpart[k] = bsum[0, rows] + bsum[1, rows] + bsum[2, rows] + bsum[3, rows]
-        spread(2, lambda k: bpart.at[k], ssum.at[me_b], b_dev, me_b, 4)
-
-    def mix_z():
-        drain(ssum, ar_recv.at[2])
-        spart[...] = (ssum[0] + ssum[1] + ssum[2] + ssum[3]).astype(BF)
-        spread(3, lambda k: spart, zsum.at[me_z], z_dev, me_z, NZ)
-
-    def mix_small_back():
-        drain(zsum, ar_recv.at[3])
-        added = zsum[0].astype(F32)
-        for z in range(1, NZ):
-            added = added + zsum[z].astype(F32)
-        total[...] = added * factor
-        spread(4, lambda k: total, sall.at[me_b], b_dev, me_b, 4)
-
-    def mix_big_back():
-        drain(sall, ar_recv.at[4])
-        spread(5, lambda k: sall, gall.at[me_c, me_a], a_dev, me_a, 4)
+            rows = slice(k * 48, (k + 1) * 48)
+            apart[k] = sum((zsum[z, rows].astype(F32) for z in range(1, NZ)), zsum[0, rows].astype(F32))
+        spread(2, lambda k: apart.at[k], asum.at[me_a], a_dev, me_a, 4)
+
+    def mix_b():
+        drain(asum, ar_recv.at[2])
+        bpart[...] = asum[0] + asum[1] + asum[2] + asum[3]
+        spread(3, lambda k: bpart, bsum.at[me_b], b_dev, me_b, 4)
+
+    def mix_z_back():
+        drain(bsum, ar_recv.at[3])
+        total[...] = (bsum[0] + bsum[1] + bsum[2] + bsum[3]) * factor
+        spread(4, lambda k: total, zall.at[me_z], z_dev, me_z, NZ)
+
+    def mix_a_back():
+        drain(zall, ar_recv.at[4])
+        spread(5, lambda k: zall, gall.at[me_c, me_a], a_dev, me_a, 4)
 
     def mix_pair_back():
         drain(gall.at[0], ar_recv.at[5])
@@ -295,13 +305,13 @@
     def mix_out():
         drain(gall.at[0], ar_recv.at[6])
         for half in range(2):
-            for lane in range(4):
-                cols = slice(lane * 128, (lane + 1) * 128)
-                for b in range(4):
-                    value = gall[half, lane, b]
-                    row = half * PIECE + b * 96
+            for q in range(NZ):
+                cols = slice((q % 4) * 128, (q % 4 + 1) * 128)
+                for a in range(4):
+                    value = gall[half, a, q]
+                    row = half * PIECE + (q // 4) * (PIECE // 2) + a * 48
                     for lo, hi, out in ((0, 512, out_mh), (512, 640, out_mw), (640, 672, out_mc)):
-                        begin, end = max(row, lo), min(row + 96, hi)
+                        begin, end = max(row, lo), min(row + 48, hi)
                         if begin < end:
                             out[begin - lo:end - lo, cols] = value[begin - row:end - row]
 
@@ -336,7 +346,7 @@
 
     def warm_on():
         drain(r.at[0], pl_recv.at[0])
-        spread_z(lambda t: r.at[0, :, t], zw.at[me_z], z_send.at[0], z_recv.at[0])
+        spread_z(lambda t: r.at[0, :, at(t)], zw.at[me_z], z_send.at[0], z_recv.at[0])
 
     def cold_on():
         drain(r_c, pl_recv.at[COLD])
@@ -361,7 +371,7 @@
 
     def partial(c, t):
         x = jnp.concatenate(
-            [r[HOT + c, 8 * j + lax.rem(i + NZ - t, NZ), t] for j in range(4) for i in range(8)], axis=0
+            [r[HOT + c, 8 * j + lax.rem(i + NZ - t, NZ), at(t)] for j in range(4) for i in range(8)], axis=0
         )
         return dot(ohh[t], x)
 
@@ -396,6 +406,9 @@
         out_th[:, cols] = value + got_l[c, 3].astype(F32) + got_s[c, 2].astype(F32)
         leave(c, out_th.at[:, cols], hbm_th.at[:, cols])
 
+    def arrive_part(n, lo, hi):
+        drain(r.at[HOT + 3, :, lo:hi], pl_recv.at[n])
+
     def arrive(c):
         drain(r.at[HOT + c], pl_recv.at[HOT + c])
 
@@ -458,14 +471,12 @@
     mix_terms()
     pl.semaphore_wait(barrier, NP - 1 + NZ - 1)
     mix_pair()
-    pack(0, term_w, 0, 1)
+    pack(0, term_w, 0, 1, mix_z, 8)
     keys(1, own_h, loc_h)
     send_labels(0, 0, 2)
     loads["w_h"].wait()
     project(up_h, w_h, term_h)
-    mix_big()
-    pack(1, term_h, HOT, 4, warm_on)
-    mix_small()
+    pack(1, term_h, HOT, 4, warm_on, 6)
     send_chunk(HOT + 1)
     drain(lr.at[0:2], lab_recv.at[0])
     sort_labels(0)
@@ -478,50 +489,55 @@
     ring(0, 0)
     send_chunk(HOT + 2)
     send_labels(1, 2, 3)
+    mix_a()
     pack_cold(1)
     ring(0, 1)
     pack_cold(2)
     pack_cold(3)
     ring(0, 2)
-    mix_z()
+    mix_b()
     arrive(1)
     ring(1, 0)
-    send_chunk(HOT + 3)
+    send_cold()
+    send_part(HOT + 3, HOT + 3, 0, 3)
+    send_part(HOT + 3, 6, 3, 8)
     ring(0, 3)
     ring(1, 1)
     ring(1, 2)
-    mix_small_back()
+    mix_z_back()
     arrive(2)
     ring(2, 0)
-    send_cold()
     ring(1, 3)
+    warm_table(0)
     ring(2, 1)
-    warm_table(0)
-    ring(2, 2)
-    mix_big_back()
-    ring_end(0)
-    arrive(3)
-    ring(3, 0)
-    ring(2, 3)
     drain(lr.at[2], lab_recv.at[1])
     sort_labels(2)
     labels_on(2, 1)
+    cold_on()
+    arrive_part(HOT + 3, 0, 3)
+    ring(3, 0)
+    ring(2, 2)
+    mix_a_back()
     ring(3, 1)
+    ring(2, 3)
+    ring_end(0)
+    arrive_part(6, 3, 8)
+    ring(3, 2)
     warm_table(1)
-    ring(3, 2)
     mix_pair_back()
-    cold_on()
+    ring_end(1)
     ring(3, 3)
-    ring_end(1)
-    ring_end(2)
     mix_out()
     leave(6, out_mh, hbm_mh)
     leave(7, out_mw, hbm_mw)
     leave(8, out_mc, hbm_mc)
+    ring_end(2)
     cold_table()
 
-    for k in range(5):
+    for k in range(4):
         drain(r.at[k, 0:NP - 1], pl_send.at[k])
+    drain(r.at[HOT + 3, 0:NP - 1, 0:3], pl_send.at[HOT + 3])
+    drain(r.at[HOT + 3, 0:NP - 1, 3:8], pl_send.at[6])
     drain(r_c.at[0:NP - 1], pl_send.at[COLD])
     drain(lr.at[0:2, 0:NP - 1], lab_send.at[0])
     drain(lr.at[2, 0:NP - 1], lab_send.at[1])
@@ -530,10 +546,10 @@
     drain(zl.at[0, 0:NZ - 1], z_send.at[2])
     drain(zl.at[1, 0:NZ - 1], z_send.at[3])
     drain(pair, ar_send.at[0])
-    drain(bsum.at[0:3], ar_send.at[1])
-    drain(ssum.at[0:3], ar_send.at[2])
-    drain(zsum.at[0:NZ - 1], ar_send.at[3])
-    drain(sall.at[0:3], ar_send.at[4])
+    drain(zsum.at[0:NZ - 1], ar_send.at[1])
+    drain(asum.at[0:3], ar_send.at[2])
+    drain(bsum.at[0:3], ar_send.at[3])
+    drain(zall.at[0:NZ - 1], ar_send.at[4])
     drain(gall.at[0, 0:3], ar_send.at[5])
     drain(gall.at[0], ar_send.at[6])
     for c in range(4):
@@ -605,10 +621,10 @@
             v((4, 4, 512, 128), BF), v((4, 3, 512, 128), BF), v((4, 4, 512, 128), BF), v((4, 3, 512, 128), BF),
             v((NZ, NP, CAP, 128), BF), v((NZ, 32, 512), BF), v((NZ, 32, 512), BF),
             v((4096, 128), BF), v((256, 4096), BF), v((128, 4096), BF),
-            v((2, 4, PIECE, 128), F32), v((4, PIECE, 128), F32), v((4, PIECE, 128), F32), v((4, PIECE, 128), F32),
-            v((4, 96, 128), F32), v((4, 96, 128), F32), v((96, 128), BF), v((NZ, 96, 128), BF), v((96, 128), F32),
-            v((4, 96, 128), F32), v((2, 4, 4, 96, 128), F32),
-            dma((9,)), dma((9,)), dma((2,)), dma((2,)), dma((6,)), dma((6,)), dma((4,)), dma((4,)),
+            v((2, NZ, PIECE // 2, 128), F32), v((NZ, PIECE // 2, 128), F32), v((NZ, PIECE // 2, 128), BF),
+            v((NZ, PIECE // 2, 128), BF), v((4, 48, 128), F32), v((4, 48, 128), F32), v((48, 128), F32),
+            v((4, 48, 128), F32), v((48, 128), F32), v((NZ, 48, 128), F32), v((2, 4, NZ, 48, 128), F32),
+            dma((9,)), dma((9,)), dma((2,)), dma((2,)), dma((7,)), dma((7,)), dma((4,)), dma((4,)),
             dma((4, 4)), dma((4, 3)), dma((4, 4)), dma((4, 3)), dma((7,)), dma((7,)),
         ],
         compiler_params=pltpu.CompilerParams(

time: 130 us -> 127 us (0.977); the launches traced: 130 us -> 124 us
  Pallas kernels: 129 us -> 124 us
    pallas_call x1, Pallas kernels: 125 us -> 120 us  [per_device(): pl.pallas_call(body, out_shape=results, in_specs=[near] * 6 + [anywhere]...]
where the time goes in v3:
time: 127 us; the launch traced here: 124 us
  Pallas kernels  124 us (98%)
    pallas_call x1, Pallas kernels, per_device(): pl.pallas_call(body, out_shape=results, in_specs=[near] * 6 + [anywhere]...  120 us
    pallas_call x1, Pallas kernels, per_device(): pl.pallas_call(write_out, out_shape=results, in_specs=[anywhere] * 6, out...  3.61 us

profile of v3, /device:TPU:2, one launch (start us, length us, event | category | flops | bytes accessed | tf_op | source)
XLA Modules:
  0.0 124.5 jit_solution(16482879811347429051)
XLA Ops:
  0.6 120.1 %shard_map.190 = (f32[512,512]{1,0:T(8,128)}, f32[2048,128]{1,0:T(8,128)}, f32[32,4096]{1,0:T(8,128)}, f32[512,512]{1,0:T(8,128)}, f32[128,512]{1,0:T(8,128)}, /*index=5*/f32[32,512]{1,0:T(8,128)}) custom-call(s32[1,2048]{1,0:T(1,128)} %bitcast.6, s32[1,2048]{1,0:T(1,128)} %bitcast.7, s32[1,2048]{1,0:T(1,128)} %bitcast.8, s32[1,2048]{1,0:T(1,128)} %bitcast.9, ...), custom_call_target="tpu_custom_call" | custom-call | tf_op jit(solution)/shard_map/pallas_call | solution.py:606
  120.7 3.6 %shard_map.191 = (f32[512,512]{1,0:T(8,128)}, f32[2048,128]{1,0:T(8,128)}, f32[32,4096]{1,0:T(8,128)}, f32[512,512]{1,0:T(8,128)}, f32[128,512]{1,0:T(8,128)}, /*index=5*/f32[32,512]{1,0:T(8,128)}) custom-call(f32[512,512]{1,0:T(8,128)} %get-tuple-element.12.refs_0_, f32[2048,128]{1,0:T(8,128)} %get-tuple-element.13.refs_1_, ...), custom_call_target="tpu_custom_call" | custom-call | tf_op jit(solution)/shard_map/pallas_call | solution.py:638

commit v4 on v3

--- a/solution.py
+++ b/solution.py
@@ -45,7 +45,7 @@
     term_w, term_c, term_h,
     tri, pick, slots, ls, lr, lz, zl,
     s, r, s_c, r_c, ohh, ring_l, ring_s, got_l, got_s,
-    zw, zc, cs, xw, ohw, lows,
+    zw, ws, zc, cs, xw, ohw, lows,
     mp, pair, part, zsum, apart, asum, bpart, bsum, total, zall, gall,
     in_sem, out_sem, lab_send, lab_recv, pl_send, pl_recv, z_send, z_recv,
     rl_send, rs_send, rl_recv, rs_recv, ar_send, ar_recv,
@@ -346,7 +346,14 @@
 
     def warm_on():
         drain(r.at[0], pl_recv.at[0])
-        spread_z(lambda t: r.at[0, :, at(t)], zw.at[me_z], z_send.at[0], z_recv.at[0])
+
+        @pl.loop(0, NZ)
+        def _(i):
+            t = lax.rem(me_z + i, NZ)
+            for p in range(NP):
+                ws[t, p] = r[0, p, at(t)]
+
+        spread_z(lambda t: ws.at[t], zw.at[me_z], z_send.at[0], z_recv.at[0])
 
     def cold_on():
         drain(r_c, pl_recv.at[COLD])
@@ -495,12 +502,12 @@
     pack_cold(2)
     pack_cold(3)
     ring(0, 2)
-    mix_b()
     arrive(1)
     ring(1, 0)
     send_cold()
     send_part(HOT + 3, HOT + 3, 0, 3)
     send_part(HOT + 3, 6, 3, 8)
+    mix_b()
     ring(0, 3)
     ring(1, 1)
     ring(1, 2)
@@ -619,7 +626,7 @@
             v((5, NP, NZ, CAP, 128), BF), v((5, NP, NZ, CAP, 128), BF), v((NP, 32, 128), BF), v((NP, 32, 128), BF),
             v((NZ, 512, 512), BF),
             v((4, 4, 512, 128), BF), v((4, 3, 512, 128), BF), v((4, 4, 512, 128), BF), v((4, 3, 512, 128), BF),
-            v((NZ, NP, CAP, 128), BF), v((NZ, 32, 512), BF), v((NZ, 32, 512), BF),
+            v((NZ, NP, CAP, 128), BF), v((NZ, NP, CAP, 128), BF), v((NZ, 32, 512), BF), v((NZ, 32, 512), BF),
             v((4096, 128), BF), v((256, 4096), BF), v((128, 4096), BF),
             v((2, NZ, PIECE // 2, 128), F32), v((NZ, PIECE // 2, 128), F32), v((NZ, PIECE // 2, 128), BF),
             v((NZ, PIECE // 2, 128), BF), v((4, 48, 128), F32), v((4, 48, 128), F32), v((48, 128), F32),

time: 127 us -> 127 us (level); the launches traced: 124 us -> 126 us
  Pallas kernels: 124 us -> 126 us
    pallas_call x1, Pallas kernels: 120 us -> 122 us  [per_device(): pl.pallas_call(body, out_shape=results, in_specs=[near] * 6 + [anywhere]...]
where the time goes in v4:
time: 127 us; the launch traced here: 126 us
  Pallas kernels  126 us (99%)
    pallas_call x1, Pallas kernels, per_device(): pl.pallas_call(body, out_shape=results, in_specs=[near] * 6 + [anywhere]...  122 us
    pallas_call x1, Pallas kernels, per_device(): pl.pallas_call(write_out, out_shape=results, in_specs=[anywhere] * 6, out...  3.61 us

profile of v4, /device:TPU:2, one launch (start us, length us, event | category | flops | bytes accessed | tf_op | source)
XLA Modules:
  0.0 126.5 jit_solution(5450892540525565374)
XLA Ops:
  0.6 122.1 %shard_map.190 = (f32[512,512]{1,0:T(8,128)}, f32[2048,128]{1,0:T(8,128)}, f32[32,4096]{1,0:T(8,128)}, f32[512,512]{1,0:T(8,128)}, f32[128,512]{1,0:T(8,128)}, /*index=5*/f32[32,512]{1,0:T(8,128)}) custom-call(s32[1,2048]{1,0:T(1,128)} %bitcast.6, s32[1,2048]{1,0:T(1,128)} %bitcast.7, s32[1,2048]{1,0:T(1,128)} %bitcast.8, s32[1,2048]{1,0:T(1,128)} %bitcast.9, ...), custom_call_target="tpu_custom_call" | custom-call | tf_op jit(solution)/shard_map/pallas_call | solution.py:613
  122.7 3.6 %shard_map.191 = (f32[512,512]{1,0:T(8,128)}, f32[2048,128]{1,0:T(8,128)}, f32[32,4096]{1,0:T(8,128)}, f32[512,512]{1,0:T(8,128)}, f32[128,512]{1,0:T(8,128)}, /*index=5*/f32[32,512]{1,0:T(8,128)}) custom-call(f32[512,512]{1,0:T(8,128)} %get-tuple-element.12.refs_0_, f32[2048,128]{1,0:T(8,128)} %get-tuple-element.13.refs_1_, ...), custom_call_target="tpu_custom_call" | custom-call | tf_op jit(solution)/shard_map/pallas_call | solution.py:645
